TPU v7x, 32 devices: a whole 2x2x4 slice. The times are simulated.
32 devices in a mesh: dp: 8 (over y, x, core), mp: 4 (over z).
Axes of the slice: x: 2, y: 2, z: 4, core: 2. Of those that a mesh axis runs over, the one named last changes fastest.
Arguments:
- tokens: bfloat16 [2048, 1024], P('dp'), may hold values from -6 to 6
- norm_gain1: float32 [1024], replicated, may hold values from 0.25 to 1.75
- in_weight: bfloat16 [1024, 3, 1024], P(None, None, 'mp'), may hold values from -0.1875 to 0.1875
- conv_taps: float32 [3, 1024], P(None, 'mp'), may hold values from -3 to 3
- out_weight: bfloat16 [1024, 1024], P('mp'), may hold values from -0.1875 to 0.1875
- norm_gain2: float32 [1024], replicated, may hold values from 0.25 to 1.75
- gate_weight: bfloat16 [1024, 4608], P(None, 'mp'), may hold values from -0.1875 to 0.1875
- up_weight: bfloat16 [1024, 4608], P(None, 'mp'), may hold values from -0.1875 to 0.1875
- down_weight: bfloat16 [4608, 1024], P('mp'), may hold values from -0.09375 to 0.09375
- cotangent: bfloat16 [2048, 1024], P('dp'), may hold values from -6 to 6
Outputs:
- block_out: bfloat16 [2048, 1024], P('dp')
- input_grad: bfloat16 [2048, 1024], P('dp')
- grad_gain1: float32 [1024], replicated
- grad_in: float32 [1024, 3, 1024], P('dp', None, 'mp')
- grad_taps: float32 [3, 1024], P(None, 'mp')
- grad_out: float32 [1024, 1024], P('mp', 'dp')
- grad_gain2: float32 [1024], replicated
- grad_gate: float32 [1024, 4608], P('dp', 'mp')
- grad_up: float32 [1024, 4608], P('dp', 'mp')
- grad_down: float32 [4608, 1024], P('mp', 'dp')
All inputs are finite; a program needn't handle non-finite values.
Results may differ from a plain program's by a relative error of at most 0.0098.
Values sent between devices are 32-bit elements; how exact they have to be, the bound alone decides.
A program may use at most 128 MiB of HBM per device.

v0:
```python
import jax
import jax.numpy as jnp
from jax import lax
from jax.sharding import PartitionSpec as P

epsilon = 1e-05


def rms_forward(values, norm_gain):
    inverse = lax.rsqrt(jnp.mean(values * values, axis=-1, keepdims=True) + epsilon)
    unit = values * inverse
    return (unit, inverse, (unit * norm_gain).astype(jnp.bfloat16))


def rms_backward(grad_normed, unit, inverse, norm_gain):
    grad_gain = jnp.sum(grad_normed * unit, axis=0)
    scaled = grad_normed * norm_gain
    grad_values = inverse * (scaled - unit * jnp.mean(scaled * unit, axis=-1, keepdims=True))
    return (grad_values, grad_gain)


def lagged(values, offset):
    return jnp.pad(values, ((offset, 0), (0, 0)))[: values.shape[0]]


def leading(values, offset):
    return jnp.pad(values, ((0, offset), (0, 0)))[offset:]


def conv_forward(mixed, conv_taps):
    total = jnp.zeros(mixed.shape, jnp.float32)
    for offset in range(conv_taps.shape[0]):
        total = total + conv_taps[offset] * lagged(mixed, offset)
    return total


def conv_backward(grad_conv, mixed, conv_taps):
    grad_mixed = jnp.zeros(mixed.shape, jnp.float32)
    rows_list = []
    for offset in range(conv_taps.shape[0]):
        grad_mixed = grad_mixed + conv_taps[offset] * leading(grad_conv, offset)
        rows_list.append(jnp.sum(grad_conv * lagged(mixed, offset), axis=0))
    return (grad_mixed, jnp.stack(rows_list))


def body(
    tokens,
    norm_gain1,
    in_weight,
    conv_taps,
    out_weight,
    norm_gain2,
    gate_weight,
    up_weight,
    down_weight,
    cotangent,
):
    length = tokens.shape[0]
    width = tokens.shape[1]
    in_flat = in_weight.reshape(width, -1)
    streams = in_flat.shape[1]
    inputs = tokens.astype(jnp.float32)
    unit1, inverse1, normed1 = rms_forward(inputs, norm_gain1)
    proj = jnp.dot(normed1, in_flat, preferred_element_type=jnp.float32).reshape(length, 3, -1)
    gate_b = proj[:, 0]
    gate_c = proj[:, 1]
    stream_x = proj[:, 2]
    mixed = gate_b * stream_x
    conved = conv_forward(mixed, conv_taps)
    gated = (gate_c * conved).astype(jnp.bfloat16)
    branch = lax.psum(jnp.dot(gated, out_weight, preferred_element_type=jnp.float32), "mp")
    resid = inputs + branch
    unit2, inverse2, normed2 = rms_forward(resid, norm_gain2)
    gate_pre = jnp.dot(normed2, gate_weight, preferred_element_type=jnp.float32)
    up_pre = jnp.dot(normed2, up_weight, preferred_element_type=jnp.float32)
    sigmoid_gate = jax.nn.sigmoid(gate_pre)
    silu_gate = gate_pre * sigmoid_gate
    hidden = (silu_gate * up_pre).astype(jnp.bfloat16)
    ffn_out = lax.psum(jnp.dot(hidden, down_weight, preferred_element_type=jnp.float32), "mp")
    block_out = (resid + ffn_out).astype(jnp.bfloat16)
    grad_down = jnp.dot(hidden.T, cotangent, preferred_element_type=jnp.float32)
    grad_hidden = jnp.dot(cotangent, down_weight.T, preferred_element_type=jnp.float32)
    grad_gpre = (
        grad_hidden * up_pre * sigmoid_gate * (1.0 + gate_pre * (1.0 - sigmoid_gate))
    ).astype(jnp.bfloat16)
    grad_upre = (grad_hidden * silu_gate).astype(jnp.bfloat16)
    grad_gate = jnp.dot(normed2.T, grad_gpre, preferred_element_type=jnp.float32)
    grad_up = jnp.dot(normed2.T, grad_upre, preferred_element_type=jnp.float32)
    partial_norm2 = jnp.dot(grad_gpre, gate_weight.T, preferred_element_type=jnp.float32) + jnp.dot(
        grad_upre, up_weight.T, preferred_element_type=jnp.float32
    )
    grad_norm2 = lax.psum(partial_norm2, "mp")
    grad_from2, grad_gain2 = rms_backward(grad_norm2, unit2, inverse2, norm_gain2)
    grad_resid = cotangent.astype(jnp.float32) + grad_from2
    resid_bf = grad_resid.astype(jnp.bfloat16)
    grad_out = jnp.dot(gated.T, resid_bf, preferred_element_type=jnp.float32)
    grad_gated = jnp.dot(resid_bf, out_weight.T, preferred_element_type=jnp.float32)
    grad_c = grad_gated * conved
    grad_conv = grad_gated * gate_c
    grad_mixed, grad_taps = conv_backward(grad_conv, mixed, conv_taps)
    grad_proj = (
        jnp.stack([grad_mixed * stream_x, grad_c, grad_mixed * gate_b], axis=1)
        .astype(jnp.bfloat16)
        .reshape(length, streams)
    )
    grad_in = jnp.dot(normed1.T, grad_proj, preferred_element_type=jnp.float32)
    grad_norm1 = lax.psum(jnp.dot(grad_proj, in_flat.T, preferred_element_type=jnp.float32), "mp")
    grad_from1, grad_gain1 = rms_backward(grad_norm1, unit1, inverse1, norm_gain1)
    input_grad = (grad_resid + grad_from1).astype(jnp.bfloat16)
    summed_in, summed_out, summed_gate, summed_up, summed_down = (
        lax.psum_scatter(grad_in, "dp", scatter_dimension=0, tiled=True),
        lax.psum_scatter(grad_out, "dp", scatter_dimension=1, tiled=True),
        lax.psum_scatter(grad_gate, "dp", scatter_dimension=0, tiled=True),
        lax.psum_scatter(grad_up, "dp", scatter_dimension=0, tiled=True),
        lax.psum_scatter(grad_down, "dp", scatter_dimension=1, tiled=True),
    )
    total_gain1, total_taps, total_gain2 = lax.psum((grad_gain1, grad_taps, grad_gain2), "dp")
    return (
        block_out,
        input_grad,
        total_gain1,
        summed_in.reshape(summed_in.shape[0], 3, -1),
        total_taps,
        summed_out,
        total_gain2,
        summed_gate,
        summed_up,
        summed_down,
    )


def solution(mesh):
    in_specs = (
        P("dp", None),
        P(),
        P(None, None, "mp"),
        P(None, "mp"),
        P("mp", None),
        P(),
        P(None, "mp"),
        P(None, "mp"),
        P("mp", None),
        P("dp", None),
    )
    out_specs = (
        P("dp", None),
        P("dp", None),
        P(),
        P("dp", None, "mp"),
        P(None, "mp"),
        P("mp", "dp"),
        P(),
        P("dp", "mp"),
        P("dp", "mp"),
        P("mp", "dp"),
    )
    return jax.shard_map(body, mesh=mesh, in_specs=in_specs, out_specs=out_specs, check_vma=False)
```

profile of v0, /device:TPU:0, one launch (start us, length us, event | category | flops | bytes accessed | tf_op | source)
XLA Modules:
  0.0 491.8 jit_solution(12263484071148346959)
XLA Ops:
  7.3 2.7 copy.21
  10.2 2.1 fusion
  15.4 54.7 %all-reduce.10.cloned.1.call-done = f32[256,1024]{1,0:T(8,128)} async-done(((f32[256,1024]{1,0:T(8,128)}), f32[256,1024]{1,0:T(8,128)}) %all-reduce.10.cloned.1.call-update) | async-done | bytes 1048592 | tf_op jit(solution)/shard_map/psum | solution.py:71
  70.1 1.7 multiply_reduce_fusion.2
  75.2 2.1 multiply_convert_fusion
  78.3 1.9 convolution_add_fusion
  80.3 2.9 fusion.35
  83.2 48.3 %all-reduce.12.cloned.1.call-done = f32[256,1024]{1,0:T(8,128)} async-done(((f32[256,1024]{1,0:T(8,128)}), f32[256,1024]{1,0:T(8,128)}) %all-reduce.12.cloned.1.call-update) | async-done | bytes 1048592 | tf_op jit(solution)/shard_map/psum | solution.py:92
  138.2 1.8 maximum_convert_fusion
  139.9 1.9 copy.22
  141.8 3.6 fusion.26
  146.3 2.5 fusion.20
  148.9 4.3 fusion.37
  153.3 4.3 fusion.38
  157.7 4.3 fusion.39
  162.6 61.1 %all-reduce.14.cloned.1.call-done = (f32[256,1024]{1,0:T(8,128)}, f32[256,1024]{1,0:T(8,128)}) async-done(((f32[256,1024]{1,0:T(8,128)}, f32[256,1024]{1,0:T(8,128)}), (f32[256,1024]{1,0:T(8,128)}, f32[256,1024]{1,0:T(8,128)})) %all-reduce.14.cloned.1.call-update) | async-done | bytes 2097168 | tf_op jit(solution)/shard_map/psum | solution.py:79
  223.7 1.8 fusion.13
  225.5 23.6 %all-reduce.4 = (f32[1024]{0:T(1024)}, f32[3,256]{1,0:T(4,128)}, f32[1024]{0:T(1024)}) all-reduce(f32[1024]{0:T(1024)S(1)} %get-tuple-element.32, f32[3,256]{1,0:T(4,128)S(1)} %pad_maximum_fusion, f32[1024]{0:T(1024)S(1)} %get-tuple-element.30), channel_id=1, replica_groups=mesh['dp'=8,'mp'=4] {'dp'}, use_global_device_ids=true, to_apply=%region_9.10 | all-reduce | flops 2816 | bytes 22528 | tf_op jit(solution)/shard_map/psum | solution.py:117
  249.2 3.3 fusion.12
  252.5 19.7 %reduce-scatter.6.cloned.1.call-done = f32[128,768]{1,0:T(8,128)} async-done(((f32[1024,768]{1,0:T(8,128)}), f32[128,768]{1,0:T(8,128)}) %reduce-scatter.6.cloned.1.call-update) | async-done | bytes 393232 | tf_op jit(solution)/shard_map/reduce_scatter | solution.py:111
  274.2 37.5 %reduce-scatter.8.cloned.1.call-done = f32[256,128]{1,0:T(8,128)} async-done(((f32[256,1024]{1,0:T(8,128)}), f32[256,128]{1,0:T(8,128)}) %reduce-scatter.8.cloned.1.call-update) | async-done | bytes 131088 | tf_op jit(solution)/shard_map/reduce_scatter | solution.py:112
  311.7 57.7 %reduce-scatter.10.cloned.1.call-done = f32[128,1152]{1,0:T(8,128)} async-done(((f32[1024,1152]{1,0:T(8,128)}), f32[128,1152]{1,0:T(8,128)}) %reduce-scatter.10.cloned.1.call-update) | async-done | bytes 589840 | tf_op jit(solution)/shard_map/reduce_scatter | solution.py:113
  369.4 57.8 %reduce-scatter.12.cloned.1.call-done = f32[128,1152]{1,0:T(8,128)} async-done(((f32[1024,1152]{1,0:T(8,128)}), f32[128,1152]{1,0:T(8,128)}) %reduce-scatter.12.cloned.1.call-update) | async-done | bytes 589840 | tf_op jit(solution)/shard_map/reduce_scatter | solution.py:114
  427.2 57.7 %reduce-scatter.14.cloned.1.call-done = f32[1152,128]{1,0:T(8,128)} async-done(((f32[1152,1024]{1,0:T(8,128)}), f32[1152,128]{1,0:T(8,128)}) %reduce-scatter.14.cloned.1.call-update) | async-done | bytes 589840 | tf_op jit(solution)/shard_map/reduce_scatter | solution.py:115
  (95 shorter events, 18.0 us)
Async XLA Ops:
  7.2 67.8 %copy-start = (bf16[1152,1024]{1,0:T(8,128)(2,1)S(1)}, bf16[1152,1024]{1,0:T(8,128)(2,1)}, u32[]{:S(2)}) copy-start(bf16[1152,1024]{1,0:T(8,128)(2,1)} %param.18) | copy-start | bytes 7077892
  7.2 2.8 copy-start.3
  7.2 3.0 copy-start.24
  7.2 62.9 %all-reduce.10.cloned.1.call-start = ((), (), s32[]{:S(2)}) async-start(), calls=%async_computation.5 | async-start | bytes 2097152 | tf_op jit(solution)/shard_map/psum | solution.py:71
  10.0 2.4 copy-start.27
  10.2 3.8 copy-start.16
  12.4 3.0 copy-start.12
  14.0 1.4 copy-start.20
  14.0 57.9 %copy-start.23 = (f32[1024]{0:T(1024)S(1)}, f32[1024]{0:T(1024)}, u32[]{:S(2)}) copy-start(f32[1024]{0:T(1024)} %param.15) | copy-start | bytes 12292
  15.3 116.2 %all-reduce.12.cloned.1.call-start = ((), (), s32[]{:S(2)}) async-start(), calls=%async_computation.6 | async-start | bytes 2097152 | tf_op jit(solution)/shard_map/psum | solution.py:92
  70.1 2.1 copy-start.5
  72.3 1.9 copy-start.4
  80.2 143.5 %all-reduce.14.cloned.1.call-start = ((), (), s32[]{:S(2)}) async-start(), calls=%async_computation.12 | async-start | bytes 4194304 | tf_op jit(solution)/shard_map/psum | solution.py:79
  131.5 1.8 copy-start.7
  131.5 1.8 copy-start.15
  133.3 1.2 copy-start.13
  133.3 1.3 copy-start.17
  134.6 1.2 copy-start.2
  134.6 1.9 copy-start.6
  138.1 134.0 %reduce-scatter.6.cloned.1.call-start = ((), (), s32[]{:S(2)}) async-start(), calls=%async_computation.7 | async-start | bytes 3538944 | tf_op jit(solution)/shard_map/reduce_scatter | solution.py:111
  145.5 166.2 %reduce-scatter.8.cloned.1.call-start = ((), (), s32[]{:S(2)}) async-start(), calls=%async_computation.8 | async-start | bytes 1179648 | tf_op jit(solution)/shard_map/reduce_scatter | solution.py:112
  148.9 220.5 %reduce-scatter.10.cloned.1.call-start = ((), (), s32[]{:S(2)}) async-start(), calls=%async_computation.9 | async-start | bytes 5308416 | tf_op jit(solution)/shard_map/reduce_scatter | solution.py:113
  153.2 274.0 %reduce-scatter.12.cloned.1.call-start = ((), (), s32[]{:S(2)}) async-start(), calls=%async_computation.10 | async-start | bytes 5308416 | tf_op jit(solution)/shard_map/reduce_scatter | solution.py:114
  157.6 327.3 %reduce-scatter.14.cloned.1.call-start = ((), (), s32[]{:S(2)}) async-start(), calls=%async_computation.11 | async-start | bytes 5308416 | tf_op jit(solution)/shard_map/reduce_scatter | solution.py:115
  (12 other events, 10.5 us)
Sparse Core Ops, SparseCore 0:
  15.5 54.6 all-reduce.9
  80.3 51.1 all-reduce.11
  138.2 85.4 all-reduce.13
  227.0 45.1 reduce-scatter.5
  275.7 35.9 reduce-scatter.7
  315.6 53.7 reduce-scatter.9
  373.4 53.7 reduce-scatter.11
  431.2 53.6 reduce-scatter.13
where the time goes:
time: 492 us
  waiting for transfers between devices  395 us (80%)
  matrix products  34.4 us (7%)
  blocking collectives  23.6 us (5%)
  between operations  14.4 us (3%)
  local copies, waits for them, and re-layouts  12.3 us (2%)
  other arithmetic  12 us (2%)
    psum x1, waiting for transfers between devices, body(): lax.psum(jnp.dot(hidden, down_weight, preferred_element_type=jnp.float32)...  61.1 us
    reduce_scatter x1, waiting for transfers between devices, body(): lax.psum_scatter(grad_up, 'dp', scatter_dimension=0, tiled=True)  57.8 us
    reduce_scatter x1, waiting for transfers between devices, body(): lax.psum_scatter(grad_down, 'dp', scatter_dimension=1, tiled=True)  57.7 us
    reduce_scatter x1, waiting for transfers between devices, body(): lax.psum_scatter(grad_gate, 'dp', scatter_dimension=0, tiled=True)  57.7 us
    psum x1, waiting for transfers between devices, body(): lax.psum(jnp.dot(gated, out_weight, preferred_element_type=jnp.float32),...  54.7 us
    psum x1, waiting for transfers between devices, body(): grad_norm2 = lax.psum(partial_norm2, 'mp')  48.3 us
    reduce_scatter x1, waiting for transfers between devices, body(): lax.psum_scatter(grad_out, 'dp', scatter_dimension=1, tiled=True)  37.5 us
    psum x1, blocking collectives, body(): lax.psum((grad_gain1, grad_taps, grad_gain2), 'dp')  23.6 us
  transfers between devices with their start and end apart: 8, of which 8 were waited for; matrix products, arithmetic and copies ran while one was open for 7% of the time, Pallas kernels for 0%

commit v1 on v0

--- a/solution.py
+++ b/solution.py
@@ -1,9 +1,359 @@
+import functools
+
 import jax
 import jax.numpy as jnp
 from jax import lax
+from jax.experimental import pallas as pl
+from jax.experimental.pallas import tpu as pltpu
 from jax.sharding import PartitionSpec as P
 
 epsilon = 1e-05
+MESH = pl.DeviceIdType.MESH
+CHUNKS = 16
+
+
+def remote(src, dst, send, recv, axis, index):
+    return pltpu.make_async_remote_copy(
+        src_ref=src,
+        dst_ref=dst,
+        send_sem=send,
+        recv_sem=recv,
+        device_id={axis: index},
+        device_id_type=MESH,
+    )
+
+
+class LineSum:
+    def __init__(self, part, out, near, across, total, sems):
+        self.part, self.out = part, out
+        self.near, self.across, self.total = near, across, total
+        self.sems = sems
+        self.me = lax.axis_index("mp")
+        self.rows = part.shape[0] // CHUNKS
+
+    def at(self, ref, k):
+        return ref.at[pl.ds(k * self.rows, self.rows), :]
+
+    def inward(self, k):
+        return remote(
+            self.at(self.part, k), self.at(self.near, k),
+            self.sems.at[0, k], self.sems.at[1, k], "mp", 1 + self.me // 3,
+        )
+
+    def swap(self, k):
+        return remote(
+            self.at(self.near, k), self.at(self.across, k),
+            self.sems.at[2, k], self.sems.at[3, k], "mp", 3 - self.me,
+        )
+
+    def outward(self, k):
+        return remote(
+            self.at(self.total, k), self.at(self.total, k),
+            self.sems.at[4, k], self.sems.at[5, k], "mp", (3 * self.me + 1) % 4,
+        )
+
+    def end_start(self):
+        for k in range(CHUNKS):
+            self.inward(k).start()
+
+    def middle_step(self, k):
+        self.inward(k).wait_recv()
+        rows = pl.ds(k * self.rows, self.rows)
+        self.near[rows, :] = self.near[rows, :] + self.part[rows, :]
+        self.swap(k).start()
+
+    def middle_close(self, k):
+        self.swap(k).wait_recv()
+        rows = pl.ds(k * self.rows, self.rows)
+        self.total[rows, :] = self.near[rows, :] + self.across[rows, :]
+        self.outward(k).start()
+        self.out[rows, :] = self.total[rows, :]
+
+    def end_finish(self):
+        for k in range(CHUNKS):
+            self.outward(k).wait_recv()
+            rows = pl.ds(k * self.rows, self.rows)
+            self.out[rows, :] = self.total[rows, :]
+        for k in range(CHUNKS):
+            self.inward(k).wait_send()
+
+    def middle_finish(self):
+        for k in range(CHUNKS):
+            self.swap(k).wait_send()
+            self.outward(k).wait_send()
+
+
+class BlockSum:
+    def __init__(self, full, out, first, second, third, sends, recvs, by_rows, start, size):
+        self.full, self.out = full, out
+        self.first, self.second, self.third = first, second, third
+        self.sends, self.recvs = sends, recvs
+        self.by_rows, self.start, self.size = by_rows, start, size
+        me = lax.axis_index("dp")
+        self.y, self.x, self.c = me // 4, (me // 2) % 2, me % 2
+        self.to_core = me + 1 - 2 * self.c
+        self.to_x = me + 2 - 4 * self.x
+        self.to_y = me + 4 - 8 * self.y
+        self.block = first.shape[1]
+        self.half = self.block // 2
+
+    def source(self, j):
+        if self.by_rows:
+            return (pl.ds(pl.multiple_of(j * self.block, self.block), self.block), pl.ds(self.start, self.size))
+        width = self.first.shape[2]
+        return (pl.ds(self.start, self.size), pl.ds(pl.multiple_of(j * width, width), width))
+
+    def target(self, h):
+        if self.by_rows:
+            return (pl.ds(h * self.half, self.half), pl.ds(self.start, self.size))
+        return (pl.ds(self.start + h * self.half, self.half), slice(None))
+
+    def part(self, h):
+        return pl.ds(h * self.half, self.half)
+
+    def copy0(self, q):
+        return remote(
+            self.full.at[self.source(2 * q + 1 - self.c)], self.first.at[q],
+            self.sends.at[q], self.recvs.at[q], "dp", self.to_core,
+        )
+
+    def copy1(self, n):
+        if n < 2:
+            src, dst = self.first.at[2 * n + 1 - self.x, self.part(0)], self.to_x
+        else:
+            src, dst = self.first.at[2 * (1 - self.y) + n - 2, self.part(1)], self.to_y
+        return remote(src, self.second.at[n], self.sends.at[4 + n], self.recvs.at[4 + n], "dp", dst)
+
+    def copy2(self, h):
+        if h == 0:
+            src, dst = self.second.at[1 - self.y], self.to_y
+        else:
+            src, dst = self.second.at[3 - self.x], self.to_x
+        return remote(src, self.third.at[h], self.sends.at[8 + h], self.recvs.at[8 + h], "dp", dst)
+
+    def stage0(self):
+        for q in range(4):
+            self.copy0(q).start()
+
+    def stage1(self):
+        for q in range(4):
+            self.copy0(q).wait_recv()
+            self.first[q] = self.first[q] + self.full[self.source(2 * q + self.c)]
+        for n in (0, 2, 1, 3):
+            self.copy1(n).start()
+
+    def stage2(self):
+        for n in range(4):
+            self.copy1(n).wait_recv()
+            if n < 2:
+                mine = self.first[2 * n + self.x, self.part(0)]
+            else:
+                mine = self.first[2 * self.y + n - 2, self.part(1)]
+            self.second[n] = self.second[n] + mine
+        for h in range(2):
+            self.copy2(h).start()
+
+    def finish(self):
+        for h in range(2):
+            self.copy2(h).wait_recv()
+            mine = self.second[self.y] if h == 0 else self.second[2 + self.x]
+            self.out[self.target(h)] = mine + self.third[h]
+
+    def drain(self):
+        for q in range(4):
+            self.copy0(q).wait_send()
+            self.copy1(q).wait_send()
+        for h in range(2):
+            self.copy2(h).wait_send()
+
+
+def greet(with_blocks):
+    barrier = pltpu.get_barrier_semaphore()
+    mp, dp = lax.axis_index("mp"), lax.axis_index("dp")
+    middle = (mp == 1) | (mp == 2)
+
+    def hello(axis, index):
+        pl.semaphore_signal(barrier, inc=1, device_id={axis: index}, device_id_type=MESH)
+
+    if with_blocks:
+        y, x, c = dp // 4, (dp // 2) % 2, dp % 2
+        hello("dp", dp + 1 - 2 * c)
+        hello("dp", dp + 2 - 4 * x)
+        hello("dp", dp + 4 - 8 * y)
+
+    @pl.when(middle)
+    def _():
+        hello("mp", 3 - mp)
+        hello("mp", 3 * (mp - 1))
+        pl.semaphore_wait(barrier, 5 if with_blocks else 2)
+
+    @pl.when(jnp.logical_not(middle))
+    def _():
+        hello("mp", 1 + mp // 3)
+        pl.semaphore_wait(barrier, 4 if with_blocks else 1)
+
+    return middle
+
+
+def traffic_kernel(n_sums, n_blocks, items, *refs):
+    refs = list(refs)
+    take = lambda n: [refs.pop(0) for _ in range(n)]
+    parts, fulls = take(n_sums), take(n_blocks)
+    outs, shards = take(n_sums), take(n_blocks)
+    line_scratch = [take(4) for _ in range(n_sums)]
+    item_scratch = [take(5) for _ in items]
+    middle = greet(n_blocks > 0)
+    sums = [LineSum(p, o, *s) for p, o, s in zip(parts, outs, line_scratch)]
+    blocks = [
+        BlockSum(fulls[which], shards[which], *scratch, by_rows, start, size)
+        for (which, by_rows, start, size), scratch in zip(items, item_scratch)
+    ]
+
+    @pl.when(jnp.logical_not(middle))
+    def _():
+        for one in sums:
+            one.end_start()
+
+    for block in blocks[:2]:
+        block.stage0()
+    for block in blocks[2:]:
+        block.stage0()
+
+    steps = [(one, k) for one in sums for k in range(CHUNKS)]
+    actions = []
+    for t in range(len(steps) + 2):
+        actions.append((steps[t] if t < len(steps) else None, steps[t - 2] if t >= 2 else None))
+
+    def run(batch):
+        @pl.when(middle)
+        def _():
+            for opening, closing in batch:
+                if opening is not None:
+                    opening[0].middle_step(opening[1])
+                if closing is not None:
+                    closing[0].middle_close(closing[1])
+
+    slots = []
+    count = len(blocks)
+    for t in range(count + 2):
+        if t < count:
+            slots.append(blocks[t].stage1)
+        if 1 <= t and t - 1 < count:
+            slots.append(blocks[t - 1].stage2)
+        if 2 <= t:
+            slots.append(blocks[t - 2].finish)
+    if not slots:
+        run(actions)
+    else:
+        done = 0
+        for position, slot in enumerate(slots):
+            slot()
+            upto = -(-len(actions) * (position + 1) // len(slots))
+            if upto > done:
+                run(actions[done:upto])
+                done = upto
+
+    @pl.when(middle)
+    def _():
+        for one in sums:
+            one.middle_finish()
+
+    @pl.when(jnp.logical_not(middle))
+    def _():
+        for one in sums:
+            one.end_finish()
+
+    for block in blocks:
+        block.drain()
+
+
+def traffic(partials, fulls, items, collective_id):
+    f32 = jnp.float32
+    scratch = []
+    for p in partials:
+        scratch += [pltpu.VMEM(p.shape, f32)] * 3 + [pltpu.SemaphoreType.DMA((6, CHUNKS))]
+    sent = sum(p.size for p in partials) * 4
+    for which, by_rows, _, size in items:
+        full = fulls[which]
+        r, c = (full.shape[0] // 8, size) if by_rows else (size, full.shape[1] // 8)
+        scratch += [
+            pltpu.VMEM((4, r, c), f32),
+            pltpu.VMEM((4, r // 2, c), f32),
+            pltpu.VMEM((2, r // 2, c), f32),
+            pltpu.SemaphoreType.DMA((10,)),
+            pltpu.SemaphoreType.DMA((10,)),
+        ]
+        sent += 7 * r * c * 4
+    kinds = {which: by_rows for which, by_rows, _, _ in items}
+    shards = [
+        jax.ShapeDtypeStruct(
+            (f.shape[0] // 8, f.shape[1]) if kinds[i] else (f.shape[0], f.shape[1] // 8), f32
+        )
+        for i, f in enumerate(fulls)
+    ]
+    vmem = pl.BlockSpec(memory_space=pltpu.VMEM)
+    n_in = len(partials) + len(fulls)
+    return pl.pallas_call(
+        functools.partial(traffic_kernel, len(partials), len(fulls), items),
+        out_shape=[jax.ShapeDtypeStruct(p.shape, f32) for p in partials] + shards,
+        in_specs=[vmem] * n_in,
+        out_specs=[vmem] * n_in,
+        scratch_shapes=scratch,
+        compiler_params=pltpu.CompilerParams(
+            collective_id=collective_id, has_side_effects=True, vmem_limit_bytes=60 * 1024 * 1024
+        ),
+        name=f"traffic_{collective_id}",
+    )(*partials, *fulls)
+
+
+def small_kernel(n, x_ref, o_ref, held, sends, recvs):
+    me = lax.axis_index("dp")
+    barrier = pltpu.get_barrier_semaphore()
+    for s in range(1, n):
+        pl.semaphore_signal(barrier, inc=1, device_id={"dp": lax.rem(me + s, n)}, device_id_type=MESH)
+    pl.semaphore_wait(barrier, n - 1)
+
+    def copy(s):
+        return remote(x_ref, held.at[me], sends.at[s], recvs.at[s], "dp", lax.rem(me + s, n))
+
+    for s in range(1, n):
+        copy(s).start()
+    held[me] = x_ref[...]
+    for s in range(1, n):
+        copy(s).wait_recv()
+    total = held[0]
+    for i in range(1, n):
+        total = total + held[i]
+    o_ref[...] = total
+    for s in range(1, n):
+        copy(s).wait_send()
+
+
+def small_sum(n, x, collective_id):
+    vmem = pl.BlockSpec(memory_space=pltpu.VMEM)
+    return pl.pallas_call(
+        functools.partial(small_kernel, n),
+        out_shape=jax.ShapeDtypeStruct(x.shape, x.dtype),
+        in_specs=[vmem],
+        out_specs=vmem,
+        scratch_shapes=[
+            pltpu.VMEM((n, *x.shape), x.dtype),
+            pltpu.SemaphoreType.DMA((n,)),
+            pltpu.SemaphoreType.DMA((n,)),
+        ],
+        compiler_params=pltpu.CompilerParams(collective_id=collective_id, has_side_effects=True),
+        name="small_sum",
+    )(x)
+
+
+def split_rows(which, size, pieces):
+    return [(which, False, i * (size // pieces), size // pieces) for i in range(pieces)]
+
+
+def split_columns(which, size, pieces):
+    lanes = size // 128
+    edges = [i * lanes // pieces * 128 for i in range(pieces)] + [size]
+    return [(which, True, a, b - a) for a, b in zip(edges, edges[1:])]
 
 
 def rms_forward(values, norm_gain):
@@ -43,7 +393,15 @@
     return (grad_mixed, jnp.stack(rows_list))
 
 
+def sums_over_mp(fast, partials, collective_id):
+    if fast:
+        return traffic(partials, [], [], collective_id)
+    return [lax.psum(p, "mp") for p in partials]
+
+
 def body(
+    parts,
+    groups,
     tokens,
     norm_gain1,
     in_weight,
@@ -68,7 +426,10 @@
     mixed = gate_b * stream_x
     conved = conv_forward(mixed, conv_taps)
     gated = (gate_c * conved).astype(jnp.bfloat16)
-    branch = lax.psum(jnp.dot(gated, out_weight, preferred_element_type=jnp.float32), "mp")
+    fast = parts == 8 and groups == 4
+    (branch,) = sums_over_mp(
+        fast, [jnp.dot(gated, out_weight, preferred_element_type=jnp.float32)], 0
+    )
     resid = inputs + branch
     unit2, inverse2, normed2 = rms_forward(resid, norm_gain2)
     gate_pre = jnp.dot(normed2, gate_weight, preferred_element_type=jnp.float32)
@@ -76,8 +437,7 @@
     sigmoid_gate = jax.nn.sigmoid(gate_pre)
     silu_gate = gate_pre * sigmoid_gate
     hidden = (silu_gate * up_pre).astype(jnp.bfloat16)
-    ffn_out = lax.psum(jnp.dot(hidden, down_weight, preferred_element_type=jnp.float32), "mp")
-    block_out = (resid + ffn_out).astype(jnp.bfloat16)
+    partial_ffn = jnp.dot(hidden, down_weight, preferred_element_type=jnp.float32)
     grad_down = jnp.dot(hidden.T, cotangent, preferred_element_type=jnp.float32)
     grad_hidden = jnp.dot(cotangent, down_weight.T, preferred_element_type=jnp.float32)
     grad_gpre = (
@@ -89,7 +449,21 @@
     partial_norm2 = jnp.dot(grad_gpre, gate_weight.T, preferred_element_type=jnp.float32) + jnp.dot(
         grad_upre, up_weight.T, preferred_element_type=jnp.float32
     )
-    grad_norm2 = lax.psum(partial_norm2, "mp")
+    if fast:
+        grad_norm2, ffn_out, summed_down, summed_gate, summed_up = traffic(
+            [partial_norm2, partial_ffn],
+            [grad_down, grad_gate, grad_up],
+            split_rows(0, grad_down.shape[0], 2)
+            + split_columns(1, grad_gate.shape[1], 2)
+            + split_columns(2, grad_up.shape[1], 2),
+            1,
+        )
+    else:
+        grad_norm2, ffn_out = lax.psum((partial_norm2, partial_ffn), "mp")
+        summed_down = lax.psum_scatter(grad_down, "dp", scatter_dimension=1, tiled=True)
+        summed_gate = lax.psum_scatter(grad_gate, "dp", scatter_dimension=0, tiled=True)
+        summed_up = lax.psum_scatter(grad_up, "dp", scatter_dimension=0, tiled=True)
+    block_out = (resid + ffn_out).astype(jnp.bfloat16)
     grad_from2, grad_gain2 = rms_backward(grad_norm2, unit2, inverse2, norm_gain2)
     grad_resid = cotangent.astype(jnp.float32) + grad_from2
     resid_bf = grad_resid.astype(jnp.bfloat16)
@@ -104,17 +478,32 @@
         .reshape(length, streams)
     )
     grad_in = jnp.dot(normed1.T, grad_proj, preferred_element_type=jnp.float32)
-    grad_norm1 = lax.psum(jnp.dot(grad_proj, in_flat.T, preferred_element_type=jnp.float32), "mp")
+    partial_norm1 = jnp.dot(grad_proj, in_flat.T, preferred_element_type=jnp.float32)
+    if fast:
+        grad_norm1, summed_in, summed_out = traffic(
+            [partial_norm1],
+            [grad_in, grad_out],
+            split_columns(0, grad_in.shape[1], 2) + split_rows(1, grad_out.shape[0], 1),
+            2,
+        )
+    else:
+        grad_norm1 = lax.psum(partial_norm1, "mp")
+        summed_in = lax.psum_scatter(grad_in, "dp", scatter_dimension=0, tiled=True)
+        summed_out = lax.psum_scatter(grad_out, "dp", scatter_dimension=1, tiled=True)
     grad_from1, grad_gain1 = rms_backward(grad_norm1, unit1, inverse1, norm_gain1)
     input_grad = (grad_resid + grad_from1).astype(jnp.bfloat16)
-    summed_in, summed_out, summed_gate, summed_up, summed_down = (
-        lax.psum_scatter(grad_in, "dp", scatter_dimension=0, tiled=True),
-        lax.psum_scatter(grad_out, "dp", scatter_dimension=1, tiled=True),
-        lax.psum_scatter(grad_gate, "dp", scatter_dimension=0, tiled=True),
-        lax.psum_scatter(grad_up, "dp", scatter_dimension=0, tiled=True),
-        lax.psum_scatter(grad_down, "dp", scatter_dimension=1, tiled=True),
-    )
-    total_gain1, total_taps, total_gain2 = lax.psum((grad_gain1, grad_taps, grad_gain2), "dp")
+    if fast:
+        small = jnp.concatenate(
+            [grad_gain1.reshape(-1, 128), grad_gain2.reshape(-1, 128), grad_taps.reshape(-1, 128)]
+        )
+        count = small.shape[0]
+        small = small_sum(parts, jnp.pad(small, ((0, -count % 8), (0, 0))), 3)
+        rows = width // 128
+        total_gain1 = small[:rows].reshape(-1)
+        total_gain2 = small[rows : 2 * rows].reshape(-1)
+        total_taps = small[2 * rows : count].reshape(grad_taps.shape)
+    else:
+        total_gain1, total_taps, total_gain2 = lax.psum((grad_gain1, grad_taps, grad_gain2), "dp")
     return (
         block_out,
         input_grad,
@@ -154,4 +543,5 @@
         P("dp", "mp"),
         P("mp", "dp"),
     )
-    return jax.shard_map(body, mesh=mesh, in_specs=in_specs, out_specs=out_specs, check_vma=False)
+    local = functools.partial(body, mesh.shape["dp"], mesh.shape["mp"])
+    return jax.shard_map(local, mesh=mesh, in_specs=in_specs, out_specs=out_specs, check_vma=False)

time: 492 us -> 227 us (0.46)
  waiting for transfers between devices: 395 us -> 0 us
  Pallas kernels: 0 us -> 157 us
  blocking collectives: 23.6 us -> 0 us
  between operations: 14.4 us -> 0.9 us
  local copies, waits for them, and re-layouts: 12.3 us -> 20.1 us
    reduce_scatter x5 -> x0, waiting for transfers between devices: 230 us -> none  [the longest x1 57.8 us: body(): lax.psum_scatter(grad_up, 'dp', scatter_dimension=0, tiled=True)]
    psum x3 -> x0, waiting for transfers between devices: 164 us -> none  [the longest x1 61.1 us: body(): lax.psum(jnp.dot(hidden, down_weight, preferred_element_type=jnp.float32)...]
    pallas_call x0 -> x4, Pallas kernels: none -> 157 us  [the longest x3 151 us: traffic(): pl.pallas_call(functools.partial(traffic_kernel, len(partials), len(fulls...]
    psum x1 -> x0, blocking collectives: 23.6 us -> none  [body(): lax.psum((grad_gain1, grad_taps, grad_gain2), 'dp')]
    unnamed x58 -> x64, local copies, waits for them, and re-layouts: 9.2 us -> 14.2 us
  transfers between devices with their start and end apart: 8 -> 0, of which waited for: 8 -> 0; matrix products, arithmetic and copies ran while one was open for 7% -> 0% of each run, Pallas kernels for 0% -> 0%
where the time goes in v1:
time: 227 us; the launch traced here: 226 us
  Pallas kernels  157 us (69%)
  matrix products  31.9 us (14%)
  local copies, waits for them, and re-layouts  20.1 us (9%)
  other arithmetic  16.3 us (7%)
    pallas_call x3, Pallas kernels, traffic(): pl.pallas_call(functools.partial(traffic_kernel, len(partials), len(fulls...  151 us
    unnamed x64, local copies, waits for them, and re-layouts  14.2 us
    pallas_call x1, Pallas kernels, small_sum(): pl.pallas_call(functools.partial(small_kernel, n), out_shape=jax.ShapeDty...  6.07 us

profile of v1, /device:TPU:0, one launch (start us, length us, event | category | flops | bytes accessed | tf_op | source)
XLA Modules:
  0.0 225.8 jit_solution(11884019194904754717)
XLA Ops:
  2.9 3.7 %fusion.33 = f32[256,1152]{1,0:T(8,128)} fusion(bf16[256,1024]{1,0:T(8,128)(2,1)} %param.19, bf16[1152,1024]{1,0:T(8,128)(2,1)} %param.18), kind=kOutput, calls=%fused_computation.70 | convolution fusion | flops 603979776 | bytes 4063232 | tf_op jit(solution)/shard_map/dot_general | solution.py:442
  6.6 2.6 %copy.21 = bf16[1024,3,256]{0,2,1:T(8,128)(2,1)} copy(bf16[1024,3,256]{2,0,1:T(8,128)(2,1)} %param.12) | data formatting | bytes 3145728 | tf_op args[2]
  9.3 2.1 fusion
  15.0 37.6 %traffic_0.1 = f32[256,1024]{1,0:T(8,128)} custom-call(f32[256,1024]{1,0:T(8,128)} %fusion.32.refs_0_), custom_call_target="tpu_custom_call" | custom-call | tf_op jit(solution)/shard_map/traffic_0/pallas_call | solution.py:296
  52.7 1.6 multiply_reduce_fusion.2
  57.6 1.9 fusion.36.refs_1_
  60.3 1.9 convolution_add_fusion.refs_0_
  62.2 3.1 %fusion.39.refs_4_ = f32[1024,1152]{1,0:T(8,128)} fusion(bf16[256,1024]{1,0:T(8,128)(2,1)S(1)} %multiply_convert_fusion.3, bf16[256,1152]{1,0:T(8,128)(2,1)S(1)} %get-tuple-element.62), kind=kOutput, calls=%fused_computation.76 | convolution fusion | flops 603979776 | bytes 5832704 | tf_op jit(solution)/shard_map/dot_general | solution.py:448
  65.3 3.1 %fusion.38.refs_3_ = f32[1024,1152]{1,0:T(8,128)} fusion(bf16[256,1024]{1,0:T(8,128)(2,1)S(1)} %multiply_convert_fusion.3, bf16[256,1152]{1,0:T(8,128)(2,1)S(1)} %get-tuple-element.61), kind=kOutput, calls=%fused_computation.75 | convolution fusion | flops 603979776 | bytes 5832704 | tf_op jit(solution)/shard_map/dot_general | solution.py:447
  68.4 2.9 %fusion.37.refs_2_ = f32[1152,1024]{1,0:T(8,128)} fusion(bf16[256,1152]{1,0:T(8,128)(2,1)S(1)} %get-tuple-element.60, bf16[256,1024]{1,0:T(8,128)(2,1)S(1)} %copy-done.7), kind=kOutput, calls=%fused_computation.74 | convolution fusion | flops 603979776 | bytes 5832704 | tf_op jit(solution)/shard_map/dot_general | solution.py:441
  71.3 75.3 %traffic_1.1 = (f32[256,1024]{1,0:T(8,128)}, f32[256,1024]{1,0:T(8,128)}, f32[1152,128]{1,0:T(8,128)}, f32[128,1152]{1,0:T(8,128)}, f32[128,1152]{1,0:T(8,128)}) custom-call(f32[256,1024]{1,0:T(8,128)} %convolution_add_fusion.refs_0_, f32[256,1024]{1,0:T(8,128)} %fusion.36.refs_1_, f32[1152,1024]{1,0:T(8,128)} %fusion.37.refs_2_, ...), custom_call_target="tpu_custom_call" | custom-call | tf_op jit(solution)/shard_map/traffic_1/pallas_call | solution.py:296
  146.6 1.7 multiply_reduce_fusion
  150.7 2.1 multiply_reduce_fusion.5
  156.7 1.9 copy.22
  158.6 3.2 %convolution_bitcast_fusion.refs_0_ = f32[256,1024]{1,0:T(8,128)} fusion(bf16[1024,3,256]{2,0,1:T(8,128)(2,1)} %param.12, bf16[256,1,256]{2,0,1:T(8,128)(2,1)S(1)} %get-tuple-element.71, bf16[256,1,256]{2,0,1:T(8,128)(2,1)} %copy-done.16, bf16[256,1,256]{2,0,1:T(8,128)(2,1)} %copy-done.17), kind=kOutput, calls=%fused_computation.9 | convolution fusion | flops 403046400 | bytes 3014656 | tf_op jit(solution)/shard_map/dot_general | solution.py:481
  163.2 2.4 %fusion.26.refs_1_ = f32[1024,768]{1,0:T(8,128)} fusion(bf16[256,768]{0,1:T(8,128)(2,1)S(1)} %bitcast.76, bf16[256,1024]{1,0:T(8,128)(2,1)S(1)} %copy-done.4, f32[1024]{0:T(1024)S(1)} %copy-done.27, f32[256]{0:T(256)S(1)} %add_rsqrt_fusion.1), kind=kOutput, calls=%fused_computation.57 | convolution fusion | flops 403701760 | bytes 4068352 | tf_op jit(solution)/shard_map/dot_general | solution.py:480
  165.6 37.6 %traffic_2.1 = (f32[256,1024]{1,0:T(8,128)}, f32[128,768]{1,0:T(8,128)}, f32[256,128]{1,0:T(8,128)}) custom-call(f32[256,1024]{1,0:T(8,128)} %convolution_bitcast_fusion.refs_0_, f32[1024,768]{1,0:T(8,128)} %fusion.26.refs_1_, f32[256,1024]{1,0:T(8,128)} %fusion.20.refs_2_), custom_call_target="tpu_custom_call" | custom-call | tf_op jit(solution)/shard_map/traffic_2/pallas_call | solution.py:296
  203.2 1.9 copy.23
  205.1 1.9 copy.24
  207.1 2.4 %fusion.13 = (f32[1024]{0:T(1024)S(1)}, f32[256]{0:T(256)}) fusion(f32[256,1024]{1,0:T(8,128)} %get-tuple-element.20, bf16[256,1024]{1,0:T(8,128)(2,1)} %param.10, f32[256]{0:T(256)S(1)} %add_rsqrt_fusion.1, f32[1024]{0:T(1024)S(1)} %copy-done.27), kind=kLoop, calls=%fused_computation.22 | loop fusion | flops 1833728 | bytes 1583104 | tf_op jit(solution)/shard_map/reduce_sum | solution.py:366
  210.1 6.1 %small_sum.1 = f32[24,128]{1,0:T(8,128)} custom-call(f32[24,128]{1,0:T(8,128)} %select_maximum_fusion.x_ref), custom_call_target="tpu_custom_call" | custom-call | tf_op jit(solution)/shard_map/small_sum/pallas_call | solution.py:334
  216.8 2.5 %fusion.12 = bf16[256,1024]{1,0:T(8,128)(2,1)} fusion(f32[256,1024]{1,0:T(8,128)S(1)} %copy-done.2, bf16[256,1024]{1,0:T(8,128)(2,1)} %param.10, f32[256,1024]{1,0:T(8,128)} %get-tuple-element.20, f32[256]{0:T(256)S(1)} %broadcast_multiply_fusion, f32[1024]{0:T(1024)} %param.11, f32[256]{0:T(256)} %copy-done.28), kind=kLoop, calls=%fused_computation.21 | loop fusion | flops 2097152 | bytes 3151872 | tf_op jit(solution)/shard_map/convert_element_type | solution.py:494
  221.2 1.9 copy.30
  223.1 1.9 copy.31
  (85 shorter events, 21.5 us)
Async XLA Ops:
  0.6 54.8 %copy-start = (bf16[1024,1152]{1,0:T(8,128)(2,1)S(1)}, bf16[1024,1152]{1,0:T(8,128)(2,1)}, u32[]{:S(2)}) copy-start(bf16[1024,1152]{1,0:T(8,128)(2,1)} %param.17) | copy-start | bytes 7077892
  2.0 205.0 %copy-start.28 = (f32[256]{0:T(256)}, f32[256]{0:T(256)S(1)}, u32[]{:S(2)}) copy-start(f32[256]{0:T(256)S(1)} %add_rsqrt_fusion.1) | copy-start | bytes 3076
  6.6 2.6 %copy-start.3 = (bf16[256,1024]{1,0:T(8,128)(2,1)S(1)}, bf16[256,1024]{1,0:T(8,128)(2,1)}, u32[]{:S(2)}) copy-start(bf16[256,1024]{1,0:T(8,128)(2,1)} %param.10) | copy-start | bytes 1572868
  6.6 2.6 %copy-start.27 = (f32[1024]{0:T(1024)S(1)}, f32[1024]{0:T(1024)}, u32[]{:S(2)}) copy-start(f32[1024]{0:T(1024)} %param.11) | copy-start | bytes 12292
  9.2 4.5 %copy-start.13 = (bf16[256,1024]{1,0:T(8,128)(2,1)S(1)}, bf16[256,1024]{1,0:T(8,128)(2,1)}, u32[]{:S(2)}) copy-start(bf16[256,1024]{1,0:T(8,128)(2,1)} %param.14) | copy-start | bytes 1572868
  15.0 39.2 %copy-start.26 = (f32[1024]{0:T(1024)S(1)}, f32[1024]{0:T(1024)}, u32[]{:S(2)}) copy-start(f32[1024]{0:T(1024)} %param.15) | copy-start | bytes 12292
  52.6 2.0 copy-start.6
  54.6 1.3 copy-start.18
  55.9 1.7 copy-start.5
  65.3 3.1 %copy-start.7 = (bf16[256,1024]{1,0:T(8,128)(2,1)S(1)}, bf16[256,1024]{1,0:T(8,128)(2,1)}, u32[]{:S(2)}) copy-start(bf16[256,1024]{1,0:T(8,128)(2,1)} %param.19) | copy-start | bytes 1572868
  146.6 1.8 copy-start.8
  146.6 1.8 copy-start.22
  148.5 2.2 copy-start.12
  148.5 2.2 copy-start.14
  149.7 3.1 %copy-start.10 = (f32[256,3,256]{2,0,1:T(8,128)S(1)}, f32[256,3,256]{2,0,1:T(8,128)}, u32[]{:S(2)}) copy-start(f32[256,3,256]{2,0,1:T(8,128)} %copy-done.9) | copy-start | bytes 2359300
  149.7 4.5 %copy-start.21 = (f32[256,256]{1,0:T(8,128)S(1)}, f32[256,256]{1,0:T(8,128)}, u32[]{:S(2)}) copy-start(f32[256,256]{1,0:T(8,128)} %get-tuple-element.59) | copy-start | bytes 786436
  155.3 6.6 %copy-start.2 = (f32[256,1024]{1,0:T(8,128)S(1)}, f32[256,1024]{1,0:T(8,128)}, u32[]{:S(2)}) copy-start(f32[256,1024]{1,0:T(8,128)} %copy-done.1) | copy-start | bytes 3145732
  158.6 3.3 %copy-start.20 = (bf16[256,256]{1,0:T(8,128)(2,1)S(1)}, bf16[256,256]{1,0:T(8,128)(2,1)}, u32[]{:S(2)}) copy-start(bf16[256,256]{1,0:T(8,128)(2,1)} %copy-done.19) | copy-start | bytes 393220
  158.6 4.6 %copy-start.4 = (bf16[256,1024]{1,0:T(8,128)(2,1)S(1)}, bf16[256,1024]{1,0:T(8,128)(2,1)}, u32[]{:S(2)}) copy-start(bf16[256,1024]{1,0:T(8,128)(2,1)} %param.10) | copy-start | bytes 1572868
  158.6 4.6 %copy-start.15 = (bf16[256,3,256]{0,2,1:T(8,128)(2,1)S(1)}, bf16[256,3,256]{0,2,1:T(8,128)(2,1)}, u32[]{:S(2)}) copy-start(bf16[256,3,256]{0,2,1:T(8,128)(2,1)} %copy.22) | copy-start | bytes 1179652
  207.1 13.5 %copy-start.24 = (f32[256,128]{1,0:T(8,128)S(1)}, f32[256,128]{1,0:T(8,128)}, u32[]{:S(2)}) copy-start(f32[256,128]{1,0:T(8,128)} %get-tuple-element.88) | copy-start | bytes 393220
  216.1 3.2 %copy-start.25 = (f32[24,128]{1,0:T(8,128)S(1)}, f32[24,128]{1,0:T(8,128)}, u32[]{:S(2)}) copy-start(f32[24,128]{1,0:T(8,128)} %small_sum.1) | copy-start | bytes 36868
  216.1 3.8 %slice-start = ((f32[24,128]{1,0:T(8,128)}), f32[6,128]{1,0:T(8,128)S(1)}, s32[]{:S(2)}) async-start(f32[24,128]{1,0:T(8,128)} %small_sum.1), calls=%async_computation | async-start | bytes 8192 | tf_op jit(solution)/shard_map/slice | solution.py:504
  219.3 5.7 %copy-start.23 = (f32[1152,128]{1,0:T(8,128)S(1)}, f32[1152,128]{1,0:T(8,128)}, u32[]{:S(2)}) copy-start(f32[1152,128]{1,0:T(8,128)} %get-tuple-element.92) | copy-start | bytes 1769476
  (6 other events, 5.1 us)

commit v2 on v1

--- a/solution.py
+++ b/solution.py
@@ -9,7 +9,7 @@
 
 epsilon = 1e-05
 MESH = pl.DeviceIdType.MESH
-CHUNKS = 16
+CHUNK_ROWS = 16
 
 
 def remote(src, dst, send, recv, axis, index):
@@ -29,7 +29,8 @@
         self.near, self.across, self.total = near, across, total
         self.sems = sems
         self.me = lax.axis_index("mp")
-        self.rows = part.shape[0] // CHUNKS
+        self.rows = CHUNK_ROWS
+        self.chunks = part.shape[0] // CHUNK_ROWS
 
     def at(self, ref, k):
         return ref.at[pl.ds(k * self.rows, self.rows), :]
@@ -53,7 +54,7 @@
         )
 
     def end_start(self):
-        for k in range(CHUNKS):
+        for k in range(self.chunks):
             self.inward(k).start()
 
     def middle_step(self, k):
@@ -70,22 +71,22 @@
         self.out[rows, :] = self.total[rows, :]
 
     def end_finish(self):
-        for k in range(CHUNKS):
+        for k in range(self.chunks):
             self.outward(k).wait_recv()
             rows = pl.ds(k * self.rows, self.rows)
             self.out[rows, :] = self.total[rows, :]
-        for k in range(CHUNKS):
+        for k in range(self.chunks):
             self.inward(k).wait_send()
 
     def middle_finish(self):
-        for k in range(CHUNKS):
+        for k in range(self.chunks):
             self.swap(k).wait_send()
             self.outward(k).wait_send()
 
 
 class BlockSum:
-    def __init__(self, full, out, first, second, third, sends, recvs, by_rows, start, size):
-        self.full, self.out = full, out
+    def __init__(self, left, right, out, mine, first, second, third, sends, recvs, by_rows, start, size):
+        self.left, self.right, self.out, self.mine = left, right, out, mine
         self.first, self.second, self.third = first, second, third
         self.sends, self.recvs = sends, recvs
         self.by_rows, self.start, self.size = by_rows, start, size
@@ -97,11 +98,15 @@
         self.block = first.shape[1]
         self.half = self.block // 2
 
-    def source(self, j):
+    def produce(self, j):
         if self.by_rows:
-            return (pl.ds(pl.multiple_of(j * self.block, self.block), self.block), pl.ds(self.start, self.size))
-        width = self.first.shape[2]
-        return (pl.ds(self.start, self.size), pl.ds(pl.multiple_of(j * width, width), width))
+            rows = pl.ds(pl.multiple_of(j * self.block, self.block), self.block)
+            columns = pl.ds(self.start, self.size)
+        else:
+            width = self.first.shape[2]
+            rows = pl.ds(self.start, self.size)
+            columns = pl.ds(pl.multiple_of(j * width, width), width)
+        return jnp.dot(self.left[rows, :], self.right[:, columns], preferred_element_type=jnp.float32)
 
     def target(self, h):
         if self.by_rows:
@@ -113,7 +118,7 @@
 
     def copy0(self, q):
         return remote(
-            self.full.at[self.source(2 * q + 1 - self.c)], self.first.at[q],
+            self.mine.at[q], self.first.at[q],
             self.sends.at[q], self.recvs.at[q], "dp", self.to_core,
         )
 
@@ -133,12 +138,13 @@
 
     def stage0(self):
         for q in range(4):
+            self.mine[q] = self.produce(2 * q + 1 - self.c)
             self.copy0(q).start()
 
     def stage1(self):
         for q in range(4):
             self.copy0(q).wait_recv()
-            self.first[q] = self.first[q] + self.full[self.source(2 * q + self.c)]
+            self.first[q] = self.first[q] + self.produce(2 * q + self.c)
         for n in (0, 2, 1, 3):
             self.copy1(n).start()
 
@@ -195,18 +201,23 @@
     return middle
 
 
-def traffic_kernel(n_sums, n_blocks, items, *refs):
+def traffic_kernel(n_sums, n_lefts, n_rights, n_shards, items, *refs):
     refs = list(refs)
     take = lambda n: [refs.pop(0) for _ in range(n)]
-    parts, fulls = take(n_sums), take(n_blocks)
-    outs, shards = take(n_sums), take(n_blocks)
+    parts, lefts, rights = take(n_sums), take(n_lefts), take(n_rights)
+    outs, shards = take(n_sums), take(n_shards)
+    turned = take(n_lefts)
     line_scratch = [take(4) for _ in range(n_sums)]
-    item_scratch = [take(5) for _ in items]
-    middle = greet(n_blocks > 0)
+    item_scratch = [take(6) for _ in items]
+    middle = greet(len(items) > 0)
     sums = [LineSum(p, o, *s) for p, o, s in zip(parts, outs, line_scratch)]
+
+    def view(shard):
+        return shards[shard] if isinstance(shard, int) else shards[shard[0]].at[shard[1]]
+
     blocks = [
-        BlockSum(fulls[which], shards[which], *scratch, by_rows, start, size)
-        for (which, by_rows, start, size), scratch in zip(items, item_scratch)
+        BlockSum(turned[left], rights[right], view(shard), *scratch, by_rows, start, size)
+        for (left, right, shard, by_rows, start, size), scratch in zip(items, item_scratch)
     ]
 
     @pl.when(jnp.logical_not(middle))
@@ -214,12 +225,16 @@
         for one in sums:
             one.end_start()
 
-    for block in blocks[:2]:
-        block.stage0()
-    for block in blocks[2:]:
-        block.stage0()
-
-    steps = [(one, k) for one in sums for k in range(CHUNKS)]
+    ready = set()
+
+    def opening(t):
+        left = items[t][0]
+        if left not in ready:
+            ready.add(left)
+            turned[left][...] = lefts[left][...].T
+        blocks[t].stage0()
+
+    steps = [(one, k) for one in sums for k in range(one.chunks)]
     actions = []
     for t in range(len(steps) + 2):
         actions.append((steps[t] if t < len(steps) else None, steps[t - 2] if t >= 2 else None))
@@ -227,31 +242,32 @@
     def run(batch):
         @pl.when(middle)
         def _():
-            for opening, closing in batch:
-                if opening is not None:
-                    opening[0].middle_step(opening[1])
-                if closing is not None:
-                    closing[0].middle_close(closing[1])
+            for first, last in batch:
+                if first is not None:
+                    first[0].middle_step(first[1])
+                if last is not None:
+                    last[0].middle_close(last[1])
 
     slots = []
     count = len(blocks)
-    for t in range(count + 2):
+    for t in range(count + 7):
         if t < count:
-            slots.append(blocks[t].stage1)
-        if 1 <= t and t - 1 < count:
-            slots.append(blocks[t - 1].stage2)
-        if 2 <= t:
-            slots.append(blocks[t - 2].finish)
-    if not slots:
-        run(actions)
-    else:
-        done = 0
-        for position, slot in enumerate(slots):
-            slot()
-            upto = -(-len(actions) * (position + 1) // len(slots))
-            if upto > done:
-                run(actions[done:upto])
-                done = upto
+            slots.append((functools.partial(opening, t), 1 if t else 0))
+        if 0 <= t - 1 < count:
+            slots.append((blocks[t - 1].stage1, 2 if t > 1 else 1))
+        if 0 <= t - 4 < count:
+            slots.append((blocks[t - 4].stage2, 2))
+        if 0 <= t - 6 < count:
+            slots.append((blocks[t - 6].finish, 2))
+    done = 0
+    for slot, weight in slots:
+        slot()
+        batch = actions[done : done + weight]
+        done += weight
+        if batch:
+            run(batch)
+    if actions[done:]:
+        run(actions[done:])
 
     @pl.when(middle)
     def _():
@@ -267,43 +283,34 @@
         block.drain()
 
 
-def traffic(partials, fulls, items, collective_id):
+def traffic(partials, lefts, rights, shards, items, collective_id):
     f32 = jnp.float32
-    scratch = []
+    scratch = [pltpu.VMEM(left.shape[::-1], left.dtype) for left in lefts]
     for p in partials:
-        scratch += [pltpu.VMEM(p.shape, f32)] * 3 + [pltpu.SemaphoreType.DMA((6, CHUNKS))]
-    sent = sum(p.size for p in partials) * 4
-    for which, by_rows, _, size in items:
-        full = fulls[which]
-        r, c = (full.shape[0] // 8, size) if by_rows else (size, full.shape[1] // 8)
+        scratch += [pltpu.VMEM(p.shape, f32)] * 3 + [pltpu.SemaphoreType.DMA((6, p.shape[0] // CHUNK_ROWS))]
+    for left, right, _, by_rows, _, size in items:
+        r, c = (lefts[left].shape[1] // 8, size) if by_rows else (size, rights[right].shape[1] // 8)
         scratch += [
+            pltpu.VMEM((4, r, c), f32),
             pltpu.VMEM((4, r, c), f32),
             pltpu.VMEM((4, r // 2, c), f32),
             pltpu.VMEM((2, r // 2, c), f32),
             pltpu.SemaphoreType.DMA((10,)),
             pltpu.SemaphoreType.DMA((10,)),
         ]
-        sent += 7 * r * c * 4
-    kinds = {which: by_rows for which, by_rows, _, _ in items}
-    shards = [
-        jax.ShapeDtypeStruct(
-            (f.shape[0] // 8, f.shape[1]) if kinds[i] else (f.shape[0], f.shape[1] // 8), f32
-        )
-        for i, f in enumerate(fulls)
-    ]
     vmem = pl.BlockSpec(memory_space=pltpu.VMEM)
-    n_in = len(partials) + len(fulls)
     return pl.pallas_call(
-        functools.partial(traffic_kernel, len(partials), len(fulls), items),
-        out_shape=[jax.ShapeDtypeStruct(p.shape, f32) for p in partials] + shards,
-        in_specs=[vmem] * n_in,
-        out_specs=[vmem] * n_in,
+        functools.partial(traffic_kernel, len(partials), len(lefts), len(rights), len(shards), items),
+        out_shape=[jax.ShapeDtypeStruct(p.shape, f32) for p in partials]
+        + [jax.ShapeDtypeStruct(shape, f32) for shape in shards],
+        in_specs=[vmem] * (len(partials) + len(lefts) + len(rights)),
+        out_specs=[vmem] * (len(partials) + len(shards)),
         scratch_shapes=scratch,
         compiler_params=pltpu.CompilerParams(
-            collective_id=collective_id, has_side_effects=True, vmem_limit_bytes=60 * 1024 * 1024
+            collective_id=collective_id, has_side_effects=True, vmem_limit_bytes=48 * 1024 * 1024
         ),
         name=f"traffic_{collective_id}",
-    )(*partials, *fulls)
+    )(*partials, *lefts, *rights)
 
 
 def small_kernel(n, x_ref, o_ref, held, sends, recvs):
@@ -346,14 +353,15 @@
     )(x)
 
 
-def split_rows(which, size, pieces):
-    return [(which, False, i * (size // pieces), size // pieces) for i in range(pieces)]
-
-
-def split_columns(which, size, pieces):
+def split_rows(left, right, shard, size, pieces):
+    step = size // pieces
+    return [(left, right, shard, False, i * step, step) for i in range(pieces)]
+
+
+def split_columns(left, right, shard, size, pieces):
     lanes = size // 128
     edges = [i * lanes // pieces * 128 for i in range(pieces)] + [size]
-    return [(which, True, a, b - a) for a, b in zip(edges, edges[1:])]
+    return [(left, right, shard, True, a, b - a) for a, b in zip(edges, edges[1:])]
 
 
 def rms_forward(values, norm_gain):
@@ -395,7 +403,7 @@
 
 def sums_over_mp(fast, partials, collective_id):
     if fast:
-        return traffic(partials, [], [], collective_id)
+        return traffic(partials, [], [], [], [], collective_id)
     return [lax.psum(p, "mp") for p in partials]
 
 
@@ -415,14 +423,12 @@
 ):
     length = tokens.shape[0]
     width = tokens.shape[1]
-    in_flat = in_weight.reshape(width, -1)
-    streams = in_flat.shape[1]
+    streams = in_weight.transpose(1, 0, 2)
     inputs = tokens.astype(jnp.float32)
     unit1, inverse1, normed1 = rms_forward(inputs, norm_gain1)
-    proj = jnp.dot(normed1, in_flat, preferred_element_type=jnp.float32).reshape(length, 3, -1)
-    gate_b = proj[:, 0]
-    gate_c = proj[:, 1]
-    stream_x = proj[:, 2]
+    gate_b, gate_c, stream_x = [
+        jnp.dot(normed1, streams[i], preferred_element_type=jnp.float32) for i in range(3)
+    ]
     mixed = gate_b * stream_x
     conved = conv_forward(mixed, conv_taps)
     gated = (gate_c * conved).astype(jnp.bfloat16)
@@ -438,58 +444,68 @@
     silu_gate = gate_pre * sigmoid_gate
     hidden = (silu_gate * up_pre).astype(jnp.bfloat16)
     partial_ffn = jnp.dot(hidden, down_weight, preferred_element_type=jnp.float32)
-    grad_down = jnp.dot(hidden.T, cotangent, preferred_element_type=jnp.float32)
     grad_hidden = jnp.dot(cotangent, down_weight.T, preferred_element_type=jnp.float32)
     grad_gpre = (
         grad_hidden * up_pre * sigmoid_gate * (1.0 + gate_pre * (1.0 - sigmoid_gate))
     ).astype(jnp.bfloat16)
     grad_upre = (grad_hidden * silu_gate).astype(jnp.bfloat16)
-    grad_gate = jnp.dot(normed2.T, grad_gpre, preferred_element_type=jnp.float32)
-    grad_up = jnp.dot(normed2.T, grad_upre, preferred_element_type=jnp.float32)
     partial_norm2 = jnp.dot(grad_gpre, gate_weight.T, preferred_element_type=jnp.float32) + jnp.dot(
         grad_upre, up_weight.T, preferred_element_type=jnp.float32
     )
     if fast:
-        grad_norm2, ffn_out, summed_down, summed_gate, summed_up = traffic(
-            [partial_norm2, partial_ffn],
-            [grad_down, grad_gate, grad_up],
-            split_rows(0, grad_down.shape[0], 2)
-            + split_columns(1, grad_gate.shape[1], 2)
-            + split_columns(2, grad_up.shape[1], 2),
+        rest = length // 2
+        ff = hidden.shape[1]
+        grad_norm2, ffn_head, summed_down, summed_gate = traffic(
+            [partial_norm2, partial_ffn[:rest]],
+            [hidden, normed2],
+            [cotangent, grad_gpre],
+            [(ff, width // parts), (width // parts, ff)],
+            split_rows(0, 0, 0, ff, 2) + split_columns(1, 1, 1, ff, 2),
             1,
         )
     else:
         grad_norm2, ffn_out = lax.psum((partial_norm2, partial_ffn), "mp")
+        grad_down = jnp.dot(hidden.T, cotangent, preferred_element_type=jnp.float32)
+        grad_gate = jnp.dot(normed2.T, grad_gpre, preferred_element_type=jnp.float32)
+        grad_up = jnp.dot(normed2.T, grad_upre, preferred_element_type=jnp.float32)
         summed_down = lax.psum_scatter(grad_down, "dp", scatter_dimension=1, tiled=True)
         summed_gate = lax.psum_scatter(grad_gate, "dp", scatter_dimension=0, tiled=True)
         summed_up = lax.psum_scatter(grad_up, "dp", scatter_dimension=0, tiled=True)
-    block_out = (resid + ffn_out).astype(jnp.bfloat16)
     grad_from2, grad_gain2 = rms_backward(grad_norm2, unit2, inverse2, norm_gain2)
     grad_resid = cotangent.astype(jnp.float32) + grad_from2
     resid_bf = grad_resid.astype(jnp.bfloat16)
-    grad_out = jnp.dot(gated.T, resid_bf, preferred_element_type=jnp.float32)
     grad_gated = jnp.dot(resid_bf, out_weight.T, preferred_element_type=jnp.float32)
     grad_c = grad_gated * conved
     grad_conv = grad_gated * gate_c
     grad_mixed, grad_taps = conv_backward(grad_conv, mixed, conv_taps)
-    grad_proj = (
-        jnp.stack([grad_mixed * stream_x, grad_c, grad_mixed * gate_b], axis=1)
-        .astype(jnp.bfloat16)
-        .reshape(length, streams)
-    )
-    grad_in = jnp.dot(normed1.T, grad_proj, preferred_element_type=jnp.float32)
-    partial_norm1 = jnp.dot(grad_proj, in_flat.T, preferred_element_type=jnp.float32)
+    grad_proj = [
+        value.astype(jnp.bfloat16) for value in (grad_mixed * stream_x, grad_c, grad_mixed * gate_b)
+    ]
+    partial_norm1 = jnp.zeros((length, width), jnp.float32)
+    for i in range(3):
+        partial_norm1 += jnp.dot(grad_proj[i], streams[i].T, preferred_element_type=jnp.float32)
     if fast:
-        grad_norm1, summed_in, summed_out = traffic(
-            [partial_norm1],
-            [grad_in, grad_out],
-            split_columns(0, grad_in.shape[1], 2) + split_rows(1, grad_out.shape[0], 1),
+        channels = gated.shape[1]
+        grad_norm1, ffn_tail, summed_up, summed_in, summed_out = traffic(
+            [partial_norm1, partial_ffn[rest:]],
+            [normed2, normed1, gated],
+            [grad_upre, *grad_proj, resid_bf],
+            [(width // parts, ff), (3, width // parts, channels), (channels, width // parts)],
+            split_columns(0, 0, 0, ff, 2)
+            + [(1, 1 + i, (1, i), True, 0, channels) for i in range(3)]
+            + split_rows(2, 4, 2, channels, 1),
             2,
         )
+        ffn_out = jnp.concatenate([ffn_head, ffn_tail])
     else:
         grad_norm1 = lax.psum(partial_norm1, "mp")
-        summed_in = lax.psum_scatter(grad_in, "dp", scatter_dimension=0, tiled=True)
+        grad_in = jnp.stack(
+            [jnp.dot(normed1.T, g, preferred_element_type=jnp.float32) for g in grad_proj]
+        )
+        grad_out = jnp.dot(gated.T, resid_bf, preferred_element_type=jnp.float32)
+        summed_in = lax.psum_scatter(grad_in, "dp", scatter_dimension=1, tiled=True)
         summed_out = lax.psum_scatter(grad_out, "dp", scatter_dimension=1, tiled=True)
+    block_out = (resid + ffn_out).astype(jnp.bfloat16)
     grad_from1, grad_gain1 = rms_backward(grad_norm1, unit1, inverse1, norm_gain1)
     input_grad = (grad_resid + grad_from1).astype(jnp.bfloat16)
     if fast:
@@ -508,7 +524,7 @@
         block_out,
         input_grad,
         total_gain1,
-        summed_in.reshape(summed_in.shape[0], 3, -1),
+        summed_in.transpose(1, 0, 2),
         total_taps,
         summed_out,
         total_gain2,

time: 227 us -> 177 us (0.78)
  matrix products: 31.9 us -> 11.5 us
  Pallas kernels: 157 us -> 146 us
  other arithmetic: 16.3 us -> 6.35 us
  local copies, waits for them, and re-layouts: 20.1 us -> 12 us
    dot_general x7 -> x6, matrix products: 18.2 us -> 4.28 us  [the longest x3 2.31 us: body(): jnp.dot(normed1, streams[i], preferred_element_type=jnp.float32)]
    pallas_call x3, Pallas kernels: 151 us -> 140 us  [traffic(): pl.pallas_call(functools.partial(traffic_kernel, len(partials), len(lefts...]
    unnamed x64 -> x37, local copies, waits for them, and re-layouts: 14.2 us -> 9.35 us
    reduce_sum x2, other arithmetic: 4.14 us -> 0.8 us  [rms_backward(): grad_gain = jnp.sum(grad_normed * unit, axis=0)]
    dot_general x1, matrix products: 3.74 us -> 0.88 us  [body(): jnp.dot(cotangent, down_weight.T, preferred_element_type=jnp.float32)]
    another operation x2 -> x0, other arithmetic: 2.45 us -> none  [body(): jnp.stack([grad_mixed * stream_x, grad_c, grad_mixed * gate_b], axis=1)]
where the time goes in v2:
time: 177 us
  Pallas kernels  146 us (82%)
  local copies, waits for them, and re-layouts  12 us (7%)
  matrix products  11.5 us (6%)
  other arithmetic  6.35 us (4%)
    pallas_call x3, Pallas kernels, traffic(): pl.pallas_call(functools.partial(traffic_kernel, len(partials), len(lefts...  140 us
    unnamed x37, local copies, waits for them, and re-layouts  9.35 us
    pallas_call x1, Pallas kernels, small_sum(): pl.pallas_call(functools.partial(small_kernel, n), out_shape=jax.ShapeDty...  6.07 us

profile of v2, /device:TPU:0, one launch (start us, length us, event | category | flops | bytes accessed | tf_op | source)
XLA Modules:
  0.0 177.0 jit_solution(8708332335124553327)
XLA Ops:
  0.7 1.4 fusion.12
  2.1 1.2 fusion.5.refs_3_
  3.6 1.0 fusion.26
  4.7 1.0 multiply_convert_fusion.7
  6.0 35.4 %traffic_0.1 = f32[256,1024]{1,0:T(8,128)S(1)} custom-call(f32[256,1024]{1,0:T(8,128)S(1)} %fusion.27.refs_0_), custom_call_target="tpu_custom_call" | custom-call | tf_op jit(solution)/shard_map/traffic_0/pallas_call | solution.py:302
  42.3 0.8 copy-done.7
  43.1 0.8 fusion.29
  44.2 0.8 copy-done.8
  45.0 0.9 fusion.28
  45.9 1.2 multiply_convert_fusion
  47.0 0.9 fusion.30
  47.9 1.8 %convolution_add_fusion.2.refs_0_ = f32[256,1024]{1,0:T(8,128)} fusion(f32[256,1024]{1,0:T(8,128)S(1)} %fusion.30, bf16[256,1152]{1,0:T(8,128)(2,1)S(1)} %get-tuple-element.44.refs_5_, bf16[1024,1152]{1,0:T(8,128)(2,1)S(1)} %copy-done), kind=kOutput, calls=%fused_computation.9 | convolution fusion | flops 604241920 | bytes 5046272 | tf_op jit(solution)/shard_map/dot_general | solution.py:452
  49.8 0.9 fusion.31
  50.8 56.8 %traffic_1.1 = (f32[256,1024]{1,0:T(8,128)S(1)}, f32[128,1024]{1,0:T(8,128)S(1)}, f32[1152,128]{1,0:T(8,128)S(1)}, f32[128,1152]{1,0:T(8,128)S(1)}) custom-call(f32[256,1024]{1,0:T(8,128)} %convolution_add_fusion.2.refs_0_, f32[128,1024]{1,0:T(8,128)S(1)} %get-tuple-element.48.refs_1_, bf16[256,1152]{1,0:T(8,128)(2,1)S(1)} %get-tuple-element.42.refs_2_, ...), custom_call_target="tpu_custom_call" | custom-call | tf_op jit(solution)/shard_map/traffic_1/pallas_call | solution.py:302
  110.6 1.3 convolution_add_fusion.refs_0_
  111.9 48.0 %traffic_2.1 = (f32[256,1024]{1,0:T(8,128)S(1)}, f32[128,1024]{1,0:T(8,128)S(1)}, f32[128,1152]{1,0:T(8,128)S(1)}, f32[3,128,256]{2,1,0:T(8,128)S(1)}, f32[256,128]{1,0:T(8,128)S(1)}) custom-call(f32[256,1024]{1,0:T(8,128)} %convolution_add_fusion.refs_0_, f32[128,1024]{1,0:T(8,128)S(1)} %get-tuple-element.47.refs_1_, ...), custom_call_target="tpu_custom_call" | custom-call | tf_op jit(solution)/shard_map/traffic_2/pallas_call | solution.py:302
  160.4 1.5 fusion.10
  162.5 6.1 %small_sum.1 = f32[24,128]{1,0:T(8,128)} custom-call(f32[24,128]{1,0:T(8,128)} %select_maximum_fusion.x_ref), custom_call_target="tpu_custom_call" | custom-call | tf_op jit(solution)/shard_map/small_sum/pallas_call | solution.py:341
  168.6 1.3 slice_bitcast_fusion.9
  171.1 1.8 %copy.25 = f32[128,3,256]{2,0,1:T(8,128)} copy(f32[128,3,256]{2,0,1:T(8,128)} %bitcast.52) | data formatting | bytes 786432
  173.0 1.6 copy.26
  174.5 0.8 copy.27
  175.4 0.8 copy.28
  176.2 0.8 copy.29
  (53 shorter events, 7.2 us)
Async XLA Ops:
  0.6 45.2 %copy-start = (bf16[1024,1152]{1,0:T(8,128)(2,1)S(1)}, bf16[1024,1152]{1,0:T(8,128)(2,1)}, u32[]{:S(2)}) copy-start(bf16[1024,1152]{1,0:T(8,128)(2,1)} %param.17) | copy-start | bytes 7077892
  0.7 2.6 %copy-start.9 = (bf16[1024,3,256]{2,0,1:T(8,128)(2,1)S(1)}, bf16[1024,3,256]{2,0,1:T(8,128)(2,1)}, u32[]{:S(2)}) copy-start(bf16[1024,3,256]{2,0,1:T(8,128)(2,1)} %param.12) | copy-start | bytes 4718596
  3.3 1.3 copy-start.15
  3.6 2.0 %copy-start.10 = (bf16[256,1024]{1,0:T(8,128)(2,1)S(1)}, bf16[256,1024]{1,0:T(8,128)(2,1)}, u32[]{:S(2)}) copy-start(bf16[256,1024]{1,0:T(8,128)(2,1)} %param.14) | copy-start | bytes 1572868
  5.7 35.8 %copy-start.6 = (bf16[256,1024]{1,0:T(8,128)(2,1)S(1)}, bf16[256,1024]{1,0:T(8,128)(2,1)}, u32[]{:S(2)}) copy-start(bf16[256,1024]{1,0:T(8,128)(2,1)} %param.10) | copy-start | bytes 1572868
  41.4 0.7 copy-start.13
  41.5 1.7 copy-start.7
  43.1 1.0 copy-start.1
  43.1 1.8 %copy-start.8 = (bf16[1152,1024]{1,0:T(8,128)(2,1)S(1)}, bf16[1152,1024]{1,0:T(8,128)(2,1)}, u32[]{:S(2)}) copy-start(bf16[1152,1024]{1,0:T(8,128)(2,1)} %param.18) | copy-start | bytes 7077892
  107.9 1.0 copy-start.11
  108.9 0.9 copy-start.12
  111.9 48.0 %copy-start.14 = (f32[1024]{0:T(1024)S(1)}, f32[1024]{0:T(1024)}, u32[]{:S(2)}) copy-start(f32[1024]{0:T(1024)} %param.11) | copy-start | bytes 12292
  159.9 2.0 %copy-start.2 = (f32[128,1152]{1,0:T(8,128)}, f32[128,1152]{1,0:T(8,128)S(1)}, u32[]{:S(2)}) copy-start(f32[128,1152]{1,0:T(8,128)S(1)} %get-tuple-element.76) | copy-start | bytes 1769476
  159.9 2.0 %copy-start.4 = (f32[3,128,256]{2,1,0:T(8,128)}, f32[3,128,256]{2,1,0:T(8,128)S(1)}, u32[]{:S(2)}) copy-start(f32[3,128,256]{2,1,0:T(8,128)S(1)} %get-tuple-element.23) | copy-start | bytes 1179652
  159.9 1.9 %copy-start.5 = (f32[256,128]{1,0:T(8,128)}, f32[256,128]{1,0:T(8,128)S(1)}, u32[]{:S(2)}) copy-start(f32[256,128]{1,0:T(8,128)S(1)} %get-tuple-element.73) | copy-start | bytes 393220
  171.1 4.2 %copy-start.3 = (f32[128,1152]{1,0:T(8,128)S(1)}, f32[128,1152]{1,0:T(8,128)}, u32[]{:S(2)}) copy-start(f32[128,1152]{1,0:T(8,128)} %copy-done.2) | copy-start | bytes 1769476

commit v3 on v2

--- a/solution.py
+++ b/solution.py
@@ -173,7 +173,7 @@
             self.copy2(h).wait_send()
 
 
-def greet(with_blocks):
+def greet(peers):
     barrier = pltpu.get_barrier_semaphore()
     mp, dp = lax.axis_index("mp"), lax.axis_index("dp")
     middle = (mp == 1) | (mp == 2)
@@ -181,7 +181,10 @@
     def hello(axis, index):
         pl.semaphore_signal(barrier, inc=1, device_id={axis: index}, device_id_type=MESH)
 
-    if with_blocks:
+    if peers == 7:
+        for s in range(1, 8):
+            hello("dp", lax.rem(dp + s, 8))
+    elif peers == 3:
         y, x, c = dp // 4, (dp // 2) % 2, dp % 2
         hello("dp", dp + 1 - 2 * c)
         hello("dp", dp + 2 - 4 * x)
@@ -191,25 +194,60 @@
     def _():
         hello("mp", 3 - mp)
         hello("mp", 3 * (mp - 1))
-        pl.semaphore_wait(barrier, 5 if with_blocks else 2)
+        pl.semaphore_wait(barrier, 2 + peers)
 
     @pl.when(jnp.logical_not(middle))
     def _():
         hello("mp", 1 + mp // 3)
-        pl.semaphore_wait(barrier, 4 if with_blocks else 1)
+        pl.semaphore_wait(barrier, 1 + peers)
 
     return middle
 
 
-def traffic_kernel(n_sums, n_lefts, n_rights, n_shards, items, *refs):
+class SmallSum:
+    def __init__(self, unit, given, out, own, held, sends, recvs):
+        self.unit, self.given, self.out = unit, given, out
+        self.own, self.held, self.sends, self.recvs = own, held, sends, recvs
+        self.me = lax.axis_index("dp")
+
+    def copy(self, s):
+        return remote(
+            self.own, self.held.at[self.me], self.sends.at[s], self.recvs.at[s],
+            "dp", lax.rem(self.me + s, 8),
+        )
+
+    def begin(self, grad):
+        gain = jnp.sum(grad[...] * self.unit[...], axis=0, keepdims=True)
+        self.own[...] = self.given[...]
+        for i in range(gain.shape[1] // 128):
+            self.own[i : i + 1, :] = gain[:, i * 128 : (i + 1) * 128]
+        for s in range(1, 8):
+            self.copy(s).start()
+        self.held[self.me] = self.own[...]
+
+    def end(self):
+        for s in range(1, 8):
+            self.copy(s).wait_recv()
+        total = self.held[0]
+        for i in range(1, 8):
+            total = total + self.held[i]
+        self.out[...] = total
+        for s in range(1, 8):
+            self.copy(s).wait_send()
+
+
+def traffic_kernel(n_sums, n_lefts, n_rights, n_shards, items, tail, *refs):
     refs = list(refs)
     take = lambda n: [refs.pop(0) for _ in range(n)]
     parts, lefts, rights = take(n_sums), take(n_lefts), take(n_rights)
+    extra = take(2) if tail else []
     outs, shards = take(n_sums), take(n_shards)
+    extra += take(1) if tail else []
     turned = take(n_lefts)
     line_scratch = [take(4) for _ in range(n_sums)]
     item_scratch = [take(6) for _ in items]
-    middle = greet(len(items) > 0)
+    small = SmallSum(*extra, *take(4)) if tail else None
+    middle = greet(7 if tail else 3 if items else 0)
     sums = [LineSum(p, o, *s) for p, o, s in zip(parts, outs, line_scratch)]
 
     def view(shard):
@@ -250,15 +288,15 @@
 
     slots = []
     count = len(blocks)
-    for t in range(count + 7):
+    for t in range(count + 4):
         if t < count:
             slots.append((functools.partial(opening, t), 1 if t else 0))
         if 0 <= t - 1 < count:
-            slots.append((blocks[t - 1].stage1, 2 if t > 1 else 1))
+            slots.append((blocks[t - 1].stage1, 1))
         if 0 <= t - 4 < count:
             slots.append((blocks[t - 4].stage2, 2))
         if 0 <= t - 6 < count:
-            slots.append((blocks[t - 6].finish, 2))
+            slots.append((blocks[t - 6].finish, 1))
     done = 0
     for slot, weight in slots:
         slot()
@@ -279,11 +317,17 @@
         for one in sums:
             one.end_finish()
 
+    if small is not None:
+        small.begin(outs[0])
+    for block in blocks[max(count - 2, 0) :]:
+        block.finish()
+    if small is not None:
+        small.end()
     for block in blocks:
         block.drain()
 
 
-def traffic(partials, lefts, rights, shards, items, collective_id):
+def traffic(partials, lefts, rights, shards, items, collective_id, tail=()):
     f32 = jnp.float32
     scratch = [pltpu.VMEM(left.shape[::-1], left.dtype) for left in lefts]
     for p in partials:
@@ -298,59 +342,56 @@
             pltpu.SemaphoreType.DMA((10,)),
             pltpu.SemaphoreType.DMA((10,)),
         ]
+    for _, given in zip(tail[:1], tail[1:]):
+        scratch += [
+            pltpu.VMEM(given.shape, f32),
+            pltpu.VMEM((8, *given.shape), f32),
+            pltpu.SemaphoreType.DMA((8,)),
+            pltpu.SemaphoreType.DMA((8,)),
+        ]
     vmem = pl.BlockSpec(memory_space=pltpu.VMEM)
     return pl.pallas_call(
-        functools.partial(traffic_kernel, len(partials), len(lefts), len(rights), len(shards), items),
+        functools.partial(
+            traffic_kernel, len(partials), len(lefts), len(rights), len(shards), items, len(tail) > 0
+        ),
         out_shape=[jax.ShapeDtypeStruct(p.shape, f32) for p in partials]
-        + [jax.ShapeDtypeStruct(shape, f32) for shape in shards],
-        in_specs=[vmem] * (len(partials) + len(lefts) + len(rights)),
-        out_specs=[vmem] * (len(partials) + len(shards)),
+        + [jax.ShapeDtypeStruct(shape, f32) for shape in shards]
+        + [jax.ShapeDtypeStruct(given.shape, f32) for given in tail[1:]],
+        in_specs=[vmem] * (len(partials) + len(lefts) + len(rights) + len(tail)),
+        out_specs=[vmem] * (len(partials) + len(shards) + len(tail[1:])),
         scratch_shapes=scratch,
         compiler_params=pltpu.CompilerParams(
             collective_id=collective_id, has_side_effects=True, vmem_limit_bytes=48 * 1024 * 1024
         ),
         name=f"traffic_{collective_id}",
-    )(*partials, *lefts, *rights)
-
-
-def small_kernel(n, x_ref, o_ref, held, sends, recvs):
-    me = lax.axis_index("dp")
-    barrier = pltpu.get_barrier_semaphore()
-    for s in range(1, n):
-        pl.semaphore_signal(barrier, inc=1, device_id={"dp": lax.rem(me + s, n)}, device_id_type=MESH)
-    pl.semaphore_wait(barrier, n - 1)
-
-    def copy(s):
-        return remote(x_ref, held.at[me], sends.at[s], recvs.at[s], "dp", lax.rem(me + s, n))
-
-    for s in range(1, n):
-        copy(s).start()
-    held[me] = x_ref[...]
-    for s in range(1, n):
-        copy(s).wait_recv()
-    total = held[0]
-    for i in range(1, n):
-        total = total + held[i]
-    o_ref[...] = total
-    for s in range(1, n):
-        copy(s).wait_send()
-
-
-def small_sum(n, x, collective_id):
+    )(*partials, *lefts, *rights, *tail)
+
+
+def hand_over_kernel(n, *refs):
+    small, gain1, gain2, taps = refs[n], refs[-3], refs[-2], refs[-1]
+    for i in range(n):
+        refs[n + 1 + i][...] = refs[i][...]
+    rows = gain1.shape[1] // 128
+    for i in range(rows):
+        gain1[:, i * 128 : (i + 1) * 128] = small[i : i + 1, :]
+        gain2[:, i * 128 : (i + 1) * 128] = small[rows + i : rows + i + 1, :]
+    per = taps.shape[1] // 128
+    for k in range(taps.shape[0]):
+        for i in range(per):
+            at = 2 * rows + k * per + i
+            taps[k : k + 1, i * 128 : (i + 1) * 128] = small[at : at + 1, :]
+
+
+def hand_over(shards, small, width, taps_shape):
     vmem = pl.BlockSpec(memory_space=pltpu.VMEM)
+    shapes = [x.shape for x in shards] + [(1, width), (1, width), taps_shape]
     return pl.pallas_call(
-        functools.partial(small_kernel, n),
-        out_shape=jax.ShapeDtypeStruct(x.shape, x.dtype),
-        in_specs=[vmem],
-        out_specs=vmem,
-        scratch_shapes=[
-            pltpu.VMEM((n, *x.shape), x.dtype),
-            pltpu.SemaphoreType.DMA((n,)),
-            pltpu.SemaphoreType.DMA((n,)),
-        ],
-        compiler_params=pltpu.CompilerParams(collective_id=collective_id, has_side_effects=True),
-        name="small_sum",
-    )(x)
+        functools.partial(hand_over_kernel, len(shards)),
+        out_shape=[jax.ShapeDtypeStruct(shape, jnp.float32) for shape in shapes],
+        in_specs=[vmem] * (len(shards) + 1),
+        out_specs=[vmem] * len(shapes),
+        name="hand_over",
+    )(*shards, small)
 
 
 def split_rows(left, right, shard, size, pieces):
@@ -460,7 +501,7 @@
             [hidden, normed2],
             [cotangent, grad_gpre],
             [(ff, width // parts), (width // parts, ff)],
-            split_rows(0, 0, 0, ff, 2) + split_columns(1, 1, 1, ff, 2),
+            split_rows(0, 0, 0, ff, 4) + split_columns(1, 1, 1, ff, 4),
             1,
         )
     else:
@@ -486,15 +527,24 @@
         partial_norm1 += jnp.dot(grad_proj[i], streams[i].T, preferred_element_type=jnp.float32)
     if fast:
         channels = gated.shape[1]
-        grad_norm1, ffn_tail, summed_up, summed_in, summed_out = traffic(
+        small = jnp.concatenate(
+            [
+                jnp.zeros((width // 128, 128), jnp.float32),
+                grad_gain2.reshape(-1, 128),
+                grad_taps.reshape(-1, 128),
+            ]
+        )
+        small = jnp.pad(small, ((0, -small.shape[0] % 8), (0, 0)))
+        grad_norm1, ffn_tail, summed_up, summed_in, summed_out, small = traffic(
             [partial_norm1, partial_ffn[rest:]],
             [normed2, normed1, gated],
             [grad_upre, *grad_proj, resid_bf],
             [(width // parts, ff), (3, width // parts, channels), (channels, width // parts)],
-            split_columns(0, 0, 0, ff, 2)
+            split_columns(0, 0, 0, ff, 4)
             + [(1, 1 + i, (1, i), True, 0, channels) for i in range(3)]
             + split_rows(2, 4, 2, channels, 1),
             2,
+            (unit1, small),
         )
         ffn_out = jnp.concatenate([ffn_head, ffn_tail])
     else:
@@ -509,15 +559,10 @@
     grad_from1, grad_gain1 = rms_backward(grad_norm1, unit1, inverse1, norm_gain1)
     input_grad = (grad_resid + grad_from1).astype(jnp.bfloat16)
     if fast:
-        small = jnp.concatenate(
-            [grad_gain1.reshape(-1, 128), grad_gain2.reshape(-1, 128), grad_taps.reshape(-1, 128)]
-        )
-        count = small.shape[0]
-        small = small_sum(parts, jnp.pad(small, ((0, -count % 8), (0, 0))), 3)
-        rows = width // 128
-        total_gain1 = small[:rows].reshape(-1)
-        total_gain2 = small[rows : 2 * rows].reshape(-1)
-        total_taps = small[2 * rows : count].reshape(grad_taps.shape)
+        shards = [summed_in, summed_out, summed_gate, summed_up, summed_down]
+        *shards, total_gain1, total_gain2, total_taps = hand_over(shards, small, width, grad_taps.shape)
+        summed_in, summed_out, summed_gate, summed_up, summed_down = shards
+        total_gain1, total_gain2 = total_gain1.reshape(-1), total_gain2.reshape(-1)
     else:
         total_gain1, total_taps, total_gain2 = lax.psum((grad_gain1, grad_taps, grad_gain2), "dp")
     return (

time: 177 us -> 182 us (1.028); the launches traced: 177 us -> 180 us
  local copies, waits for them, and re-layouts: 12 us -> 8.93 us
  other arithmetic: 6.35 us -> 9.29 us
    pallas_call x3, Pallas kernels: 140 us -> 144 us  [traffic(): pl.pallas_call(functools.partial(traffic_kernel, len(partials), len(lefts...]
    unnamed x37 -> x76, local copies, waits for them, and re-layouts: 9.35 us -> 5.34 us
    pallas_call x1, Pallas kernels: 6.07 us -> 3.01 us  [hand_over(): pl.pallas_call(functools.partial(hand_over_kernel, len(shards)), out_shap...]
    convert_element_type x2, other arithmetic: 0.13 us -> 2.33 us  [body(): value.astype(jnp.bfloat16)]
    dot_general x1, matrix products: 0.88 us -> 2.76 us  [body(): jnp.dot(cotangent, down_weight.T, preferred_element_type=jnp.float32)]
    reshape x2 -> x0, local copies, waits for them, and re-layouts: 1.88 us -> none  [the longest x1 1.28 us: body(): total_gain2 = small[rows:2 * rows].reshape(-1)]
where the time goes in v3:
time: 182 us; the launch traced here: 180 us
  Pallas kernels  147 us (81%)
  matrix products  13.3 us (7%)
  other arithmetic  9.29 us (5%)
  local copies, waits for them, and re-layouts  8.93 us (5%)
    pallas_call x3, Pallas kernels, traffic(): pl.pallas_call(functools.partial(traffic_kernel, len(partials), len(lefts...  144 us
    unnamed x76, local copies, waits for them, and re-layouts  5.34 us

profile of v3, /device:TPU:0, one launch (start us, length us, event | category | flops | bytes accessed | tf_op | source)
XLA Modules:
  0.0 180.0 jit_solution(1651807783545178537)
XLA Ops:
  1.3 1.3 fusion.1
  2.6 0.8 fusion.14
  3.4 2.8 %fusion.17 = f32[256,1152]{1,0:T(8,128)S(1)} fusion(bf16[256,1024]{1,0:T(8,128)(2,1)} %refs_4_.1, bf16[1152,1024]{1,0:T(8,128)(2,1)} %param.18), kind=kOutput, calls=%fused_computation.56 | convolution fusion | flops 603979776 | bytes 4063232 | tf_op jit(solution)/shard_map/dot_general | solution.py:488
  6.3 1.2 convert_multiply_fusion
  8.4 1.0 fusion.15
  10.0 35.4 %traffic_0.1 = f32[256,1024]{1,0:T(8,128)S(1)} custom-call(f32[256,1024]{1,0:T(8,128)S(1)} %fusion.16.refs_0_), custom_call_target="tpu_custom_call" | custom-call | tf_op jit(solution)/shard_map/traffic_0/pallas_call | solution.py:353
  46.3 1.2 copy-done.24
  47.5 0.8 fusion.18
  48.4 1.1 multiply_convert_fusion
  50.1 0.8 fusion.20
  50.9 0.9 fusion.13
  51.8 0.9 fusion.19
  52.7 1.8 %convolution_add_fusion.2.refs_0_ = f32[256,1024]{1,0:T(8,128)} fusion(f32[256,1024]{1,0:T(8,128)S(1)} %fusion.19, bf16[256,1152]{1,0:T(8,128)(2,1)S(1)} %get-tuple-element.60.refs_5_, bf16[1024,1152]{1,0:T(8,128)(2,1)S(1)} %copy-done), kind=kOutput, calls=%fused_computation.5 | convolution fusion | flops 604241920 | bytes 5046272 | tf_op jit(solution)/shard_map/dot_general | solution.py:493
  54.6 49.4 %traffic_1.1 = (f32[256,1024]{1,0:T(8,128)S(1)}, f32[128,1024]{1,0:T(8,128)S(1)}, f32[1152,128]{1,0:T(8,128)S(1)}, f32[128,1152]{1,0:T(8,128)S(1)}) custom-call(f32[256,1024]{1,0:T(8,128)} %convolution_add_fusion.2.refs_0_, f32[128,1024]{1,0:T(8,128)S(1)} %get-tuple-element.64.refs_1_, bf16[256,1152]{1,0:T(8,128)(2,1)S(1)} %get-tuple-element.58.refs_2_, ...), custom_call_target="tpu_custom_call" | custom-call | tf_op jit(solution)/shard_map/traffic_1/pallas_call | solution.py:353
  105.5 1.1 multiply_reduce_fusion.6
  107.3 1.3 reshape.59
  108.6 0.9 pad_maximum_fusion
  109.5 1.4 multiply_convert_fusion.5
  110.8 1.0 multiply_convert_fusion.7.refs_6_
  112.5 1.3 convolution_add_fusion.refs_0_
  114.2 59.5 %traffic_2.1 = (f32[256,1024]{1,0:T(8,128)S(1)}, f32[128,1024]{1,0:T(8,128)S(1)}, f32[128,1152]{1,0:T(8,128)S(1)}, f32[3,128,256]{2,1,0:T(8,128)S(1)}, f32[256,128]{1,0:T(8,128)S(1)}, /*index=5*/f32[24,128]{1,0:T(8,128)S(1)}) custom-call(f32[256,1024]{1,0:T(8,128)} %convolution_add_fusion.refs_0_, f32[128,1024]{1,0:T(8,128)S(1)} %copy-done.9, ...), custom_call_target="tpu_custom_call" | custom-call | tf_op jit(solution)/shard_map/traffic_2/pallas_call | solution.py:353
  174.0 1.2 copy-done.2
  175.4 1.6 add_convert_fusion
  177.0 3.0 %hand_over.1 = (f32[3,128,256]{2,1,0:T(8,128)}, f32[256,128]{1,0:T(8,128)}, f32[128,1152]{1,0:T(8,128)}, f32[128,1152]{1,0:T(8,128)}, f32[1152,128]{1,0:T(8,128)...) custom-call(f32[3,128,256]{2,1,0:T(8,128)} %copy-done.16, f32[256,128]{1,0:T(8,128)} %copy-done.17, ...), custom_call_target="tpu_custom_call" | custom-call | tf_op jit(solution)/shard_map/hand_over/pallas_call | solution.py:388
  (92 shorter events, 7.1 us)
Async XLA Ops:
  0.6 47.7 %copy-start = (bf16[1024,1152]{1,0:T(8,128)(2,1)S(1)}, bf16[1024,1152]{1,0:T(8,128)(2,1)}, u32[]{:S(2)}) copy-start(bf16[1024,1152]{1,0:T(8,128)(2,1)} %param.17) | copy-start | bytes 7077892
  2.6 3.6 %copy-start.31 = (f32[256]{0:T(256)}, f32[256]{0:T(256)S(1)}, u32[]{:S(2)}) copy-start(f32[256]{0:T(256)S(1)} %add_rsqrt_fusion.1) | copy-start | bytes 3076
  3.4 6.0 %copy-start.33 = (f32[1,256]{1,0:T(1,128)}, f32[1,256]{1,0:T(1,128)S(1)}, u32[]{:S(2)}) copy-start(f32[1,256]{1,0:T(1,128)S(1)} %get-tuple-element.68) | copy-start | bytes 3076
  3.4 6.0 %copy-start.34 = (f32[1,256]{1,0:T(1,128)}, f32[1,256]{1,0:T(1,128)S(1)}, u32[]{:S(2)}) copy-start(f32[1,256]{1,0:T(1,128)S(1)} %get-tuple-element.69) | copy-start | bytes 3076
  3.4 6.0 %copy-start.35 = (f32[1,256]{1,0:T(1,128)}, f32[1,256]{1,0:T(1,128)S(1)}, u32[]{:S(2)}) copy-start(f32[1,256]{1,0:T(1,128)S(1)} %get-tuple-element.70) | copy-start | bytes 3076
  3.4 2.8 %copy-start.21 = (bf16[256,1024]{1,0:T(8,128)(2,1)S(1)}, bf16[256,1024]{1,0:T(8,128)(2,1)}, u32[]{:S(2)}) copy-start(bf16[256,1024]{1,0:T(8,128)(2,1)} %param.10) | copy-start | bytes 1572868
  3.4 2.8 %copy-start.30 = (f32[1024]{0:T(1024)S(1)}, f32[1024]{0:T(1024)}, u32[]{:S(2)}) copy-start(f32[1024]{0:T(1024)} %param.11) | copy-start | bytes 12292
  6.2 1.8 copy-start.25
  45.5 2.1 %copy-start.24 = (bf16[1024,1152]{1,0:T(8,128)(2,1)S(1)}, bf16[1024,1152]{1,0:T(8,128)(2,1)}, u32[]{:S(2)}) copy-start(bf16[1024,1152]{1,0:T(8,128)(2,1)} %param.16) | copy-start | bytes 7077892
  45.7 58.7 %copy-start.19 = (f32[256,1024]{1,0:T(8,128)}, f32[256,1024]{1,0:T(8,128)S(1)}, u32[]{:S(2)}) copy-start(f32[256,1024]{1,0:T(8,128)S(1)} %get-tuple-element.55) | copy-start | bytes 3145732
  49.5 3.2 %copy-start.7 = (bf16[256,1152]{1,0:T(8,128)(2,1)}, bf16[256,1152]{1,0:T(8,128)(2,1)S(1)}, u32[]{:S(2)}) copy-start(bf16[256,1152]{1,0:T(8,128)(2,1)S(1)} %get-tuple-element.60.refs_5_) | copy-start | bytes 1769476
  52.7 1.9 %copy-start.3 = (bf16[256,1024]{1,0:T(8,128)(2,1)S(1)}, bf16[256,1024]{1,0:T(8,128)(2,1)}, u32[]{:S(2)}) copy-start(bf16[256,1024]{1,0:T(8,128)(2,1)} %refs_4_.1) | copy-start | bytes 1572868
  108.6 3.2 %copy-start.26 = (bf16[1024,3,256]{2,0,1:T(8,128)(2,1)S(1)}, bf16[1024,3,256]{2,0,1:T(8,128)(2,1)}, u32[]{:S(2)}) copy-start(bf16[1024,3,256]{2,0,1:T(8,128)(2,1)} %param.12) | copy-start | bytes 4718596
  109.5 2.7 %copy-start.10 = (bf16[256,256]{1,0:T(8,128)(2,1)S(1)}, bf16[256,256]{1,0:T(8,128)(2,1)}, u32[]{:S(2)}) copy-start(bf16[256,256]{1,0:T(8,128)(2,1)} %get-tuple-element.67.refs_7_) | copy-start | bytes 393220
  114.1 59.5 %copy-start.22 = (bf16[256,1024]{1,0:T(8,128)(2,1)S(1)}, bf16[256,1024]{1,0:T(8,128)(2,1)}, u32[]{:S(2)}) copy-start(bf16[256,1024]{1,0:T(8,128)(2,1)} %param.10) | copy-start | bytes 1572868
  114.1 59.6 %copy-start.32 = (f32[256]{0:T(256)S(1)}, f32[256]{0:T(256)}, u32[]{:S(2)}) copy-start(f32[256]{0:T(256)} %copy-done.31) | copy-start | bytes 3076
  114.1 59.9 %copy-start.15 = (f32[128,1024]{1,0:T(8,128)S(1)}, f32[128,1024]{1,0:T(8,128)}, u32[]{:S(2)}) copy-start(f32[128,1024]{1,0:T(8,128)} %copy-done.14) | copy-start | bytes 1572868
  114.1 59.9 %copy-start.20 = (f32[256,1024]{1,0:T(8,128)S(1)}, f32[256,1024]{1,0:T(8,128)}, u32[]{:S(2)}) copy-start(f32[256,1024]{1,0:T(8,128)} %copy-done.19) | copy-start | bytes 3145732
  173.6 3.4 %copy-start.13 = (f32[128,1152]{1,0:T(8,128)}, f32[128,1152]{1,0:T(8,128)S(1)}, u32[]{:S(2)}) copy-start(f32[128,1152]{1,0:T(8,128)S(1)} %get-tuple-element.35.refs_3_) | copy-start | bytes 1769476
  173.6 3.4 %copy-start.16 = (f32[3,128,256]{2,1,0:T(8,128)}, f32[3,128,256]{2,1,0:T(8,128)S(1)}, u32[]{:S(2)}) copy-start(f32[3,128,256]{2,1,0:T(8,128)S(1)} %get-tuple-element.32.refs_0_) | copy-start | bytes 1179652
  173.6 3.4 %copy-start.17 = (f32[256,128]{1,0:T(8,128)}, f32[256,128]{1,0:T(8,128)S(1)}, u32[]{:S(2)}) copy-start(f32[256,128]{1,0:T(8,128)S(1)} %get-tuple-element.33.refs_1_) | copy-start | bytes 393220
  173.6 3.3 %copy-start.18 = (f32[24,128]{1,0:T(8,128)}, f32[24,128]{1,0:T(8,128)S(1)}, u32[]{:S(2)}) copy-start(f32[24,128]{1,0:T(8,128)S(1)} %get-tuple-element.37.refs_5_) | copy-start | bytes 36868
  173.7 1.7 copy-start.4
  173.7 1.7 copy-start.37
  (14 other events, 17.9 us)
